TPU v7x, 32 devices: a whole 2x2x4 slice. The times are simulated.
32 devices in a mesh: grp: 4 (over y, x), ep: 8 (over z, core).
Axes of the slice: x: 2, y: 2, z: 4, core: 2. Of those that a mesh axis runs over, the one named last changes fastest.
Arguments:
- token_ids: int32 [4, 8, 256], P('grp'), may hold values from 0 to 49215
- expert_routes: int32 [4, 8, 256, 8], P('grp', 'ep'), may hold values from 0 to 31, all different within a row; in each aligned block of 256 rows (0 to 255, 256 to 511, ..., all dimensions but the last counted through in order) at most 96 rows name the same one
- route_weights: float32 [4, 8, 256, 8], P('grp', 'ep'), may hold values from 0.2 to 0.8
- action_positions: int32 [4, 8, 32], P('grp', 'ep'), may hold values from 0 to 255
- action_tokens: int32 [4, 8, 32], P('grp'), may hold values from 0 to 49215
- advantages: float32 [4, 8, 32], P('grp'), may hold values from -5 to 5
- value_targets: float32 [4, 8, 32], P('grp', 'ep'), may hold values from -5 to 5
- owners: int32 [3843], replicated, may hold values from 0 to 3, as said below
- master_weights: float32 [7688, 8, 4096], P('grp', 'ep'), as said below
- first_moment: float32 [7688, 8, 4096], P('grp', 'ep'), as said below
- second_moment: float32 [7688, 8, 4096], P('grp', 'ep'), as said below
Outputs:
- loss: float32 [], replicated
- grad_norm: float32 [], replicated
- new_master: float32 [7688, 8, 4096], P('grp', 'ep')
- new_first: float32 [7688, 8, 4096], P('grp', 'ep')
- new_second: float32 [7688, 8, 4096], P('grp', 'ep')
Inputs may be any that keep to these rules, and one draw needn't show every extreme that they name: `owners`: each index of grp owns at most 1922 blocks, and one owns exactly 1922. `expert_routes`: each token names 8 different experts; among the routes of one device's 256 tokens no expert is named more than 96 times, and some expert is named that often. `master_weights`: padding rows are zero; the attention part's blocks are equal in every column. `first_moment`: padding rows are zero; the attention part's blocks are equal in every column. `second_moment`: padding rows are zero, all others positive; the attention part's blocks are equal in every column.
All inputs are finite; a program needn't handle non-finite values.
Results may differ from a plain program's by a relative error of at most 0.014.
The roundings to bfloat16 on the way count: a program that leaves them out, or rounds other values in their place, can miss the bound.
Values may be sent and summed in bfloat16 or wider, within the bound.
No kernel may reach another device: no remote copies, remote signals or barrier semaphores. Data moves between devices by JAX's collectives and lax.ppermute only.
A program may use at most 576 MiB of HBM per device.

v0:
```python
import math

import jax
import jax.numpy as jnp
from jax import lax
from jax.sharding import PartitionSpec as P

D = 1024
HEADS = 16
KV = 8
HD = 64
FF = 512
EXPERTS = 32
TOP = 8
VOCAB = 49216
ADAM_STEP = 10
CAP_EXP = 96


NORM_EPS = 1e-06
VALUE_COEF = 0.5
CLIP_BASE = 24.0
LEARN_RATE = 0.01
BETA_ONE = 0.9
BETA_TWO = 0.95
ADAM_EPS = 1e-08
WEIGHT_DECAY = 0.1
ROPE_BASE = 10000.0
MASK_FILL = -1e30


def combined_all(value, axis, combine):
    everything = jax.tree.map(lambda part: lax.all_gather(part, axis), value)
    initial = jax.tree.map(lambda part: part[0], everything)

    def turn(k, so_far):
        return combine(so_far, jax.tree.map(lambda part: part[k], everything))

    return lax.fori_loop(1, lax.axis_size(axis), turn, initial)


def rms_norm(values, gain_row):
    return (
        values * lax.rsqrt(jnp.mean(values * values, axis=-1, keepdims=True) + NORM_EPS) * gain_row
    )


def rope_tables(length):
    positions = jnp.arange(length).astype(jnp.float32)
    inverse = ROPE_BASE ** (-2.0 * jnp.arange(HD // 2).astype(jnp.float32) / HD)
    angles = positions[:, None] * inverse[None, :]
    return (jnp.cos(angles)[:, None, :], jnp.sin(angles)[:, None, :])


def rotate(values, cosine, sine_table):
    half_size = values.shape[-1] // 2
    front = values[..., :half_size]
    behind = values[..., half_size:]
    return jnp.concatenate(
        [front * cosine - behind * sine_table, behind * cosine + front * sine_table], axis=-1
    )


def rotate_back(values, cosine, sine_table):
    half_size = values.shape[-1] // 2
    front = values[..., :half_size]
    behind = values[..., half_size:]
    return jnp.concatenate(
        [front * cosine + behind * sine_table, behind * cosine - front * sine_table], axis=-1
    )


def slot_tables(routes):
    flat_routes = routes.reshape(-1)
    pairs = flat_routes.shape[0]
    member = (flat_routes[:, None] == jnp.arange(EXPERTS, dtype=jnp.int32)[None, :]).astype(
        jnp.int32
    )
    ranking = jnp.sum((jnp.cumsum(member, axis=0) - member) * member, axis=1)
    pair_slot = flat_routes * CAP_EXP + ranking
    slot_pair = (
        jnp.full((EXPERTS * CAP_EXP,), pairs, jnp.int32)
        .at[pair_slot]
        .set(jnp.arange(pairs, dtype=jnp.int32))
    )
    return (pair_slot, slot_pair)


def combine_stats(earlier, later):
    top_score = jnp.maximum(earlier[0], later[0])
    mass = earlier[1] * jnp.exp(earlier[0] - top_score) + later[1] * jnp.exp(later[0] - top_score)
    return (top_score, mass, earlier[2] + later[2])


def on_device(
    token_ids,
    expert_routes,
    route_weights,
    action_positions,
    action_tokens,
    advantages,
    value_targets,
    owners,
    master_weights,
    first_moment,
    second_moment,
):
    groups = lax.axis_size("grp")
    shards = lax.axis_size("ep")
    group_index = lax.axis_index("grp")
    shard_index = lax.axis_index("ep")
    capacity = master_weights.shape[0]
    row_width = master_weights.shape[2]
    blocks = owners.shape[0]
    length = token_ids.shape[2]
    act_count = action_positions.shape[2]
    local_experts = EXPERTS // shards
    vocab_rows = VOCAB // shards
    npos = groups * shards * act_count
    groups_per = HEADS // KV
    embed_scale = math.sqrt(D) / 2.0
    gu_size = local_experts * D * 2 * FF
    dn_size = local_experts * FF * D
    col_size = gu_size + dn_size + vocab_rows * D
    query_end = col_size + D * HEADS * HD
    keyval_end = query_end + D * 2 * KV * HD
    out_end = keyval_end + HEADS * HD * D
    member = (owners[:, None] == jnp.arange(groups, dtype=jnp.int32)[None, :]).astype(jnp.int32)
    ranking = jnp.sum((jnp.cumsum(member, axis=0) - member) * member, axis=1)
    row_of_block = owners * capacity + ranking
    block_of_row = (
        jnp.full((groups * capacity,), blocks, jnp.int32)
        .at[row_of_block]
        .set(jnp.arange(blocks, dtype=jnp.int32))
    )
    gathered = lax.all_gather(
        master_weights.reshape(capacity, row_width).astype(jnp.bfloat16), "grp", axis=0, tiled=True
    )
    column = gathered[row_of_block].reshape(-1)
    gate_up = column[:gu_size].reshape(local_experts, D, 2 * FF)
    down = column[gu_size : gu_size + dn_size].reshape(local_experts, FF, D)
    table = column[gu_size + dn_size : col_size].reshape(vocab_rows, D)
    w_query = column[col_size:query_end].reshape(D, HEADS * HD)
    w_keyval = column[query_end:keyval_end].reshape(D, 2 * KV * HD)
    w_out = column[keyval_end:out_end].reshape(HEADS * HD, D)
    gains = column[out_end : out_end + 4 * D].reshape(4, D).astype(jnp.float32)
    group_ids = token_ids.reshape(shards * length)
    local_ids = group_ids - shard_index * vocab_rows
    inside = (local_ids >= 0) & (local_ids < vocab_rows)
    safe_ids = jnp.clip(local_ids, 0, vocab_rows - 1)
    found = jnp.where(inside[:, None], table[safe_ids], jnp.zeros((), jnp.bfloat16))
    x_embed = embed_scale * lax.psum_scatter(found, "ep", scatter_dimension=0, tiled=True).astype(
        jnp.float32
    )
    cosine, sine_table = rope_tables(length)
    score_scale = HD ** (-0.5)
    causal = jnp.arange(length)[:, None] >= jnp.arange(length)[None, :]
    normed = rms_norm(x_embed, gains[0]).astype(jnp.bfloat16)
    query = jnp.dot(normed, w_query, preferred_element_type=jnp.float32).reshape(length, HEADS, HD)
    keyval = jnp.dot(normed, w_keyval, preferred_element_type=jnp.float32).reshape(
        length, 2, KV, HD
    )
    query_low = (
        rotate(query, cosine, sine_table).astype(jnp.bfloat16).reshape(length, KV, groups_per, HD)
    )
    keys_low = rotate(keyval[:, 0], cosine, sine_table).astype(jnp.bfloat16)
    values_low = keyval[:, 1].astype(jnp.bfloat16)

    def score_block():
        scores = (
            jnp.einsum("tkgd,skd->kgts", query_low, keys_low, preferred_element_type=jnp.float32)
            * score_scale
        )
        return jnp.where(causal, scores, MASK_FILL)

    scores = score_block()
    peak_score = jnp.max(scores, axis=-1, keepdims=True)
    expo = jnp.exp(scores - peak_score)
    denom = jnp.sum(expo, axis=-1, keepdims=True)
    log_denom = peak_score + jnp.log(denom)
    probs_low = (expo / denom).astype(jnp.bfloat16)
    attended = jnp.einsum(
        "kgts,skd->tkgd", probs_low, values_low, preferred_element_type=jnp.float32
    )
    attended = attended.reshape(length, HEADS * HD).astype(jnp.bfloat16)
    x_attn = x_embed + jnp.dot(attended, w_out, preferred_element_type=jnp.float32)
    pair_slot, slot_pair = slot_tables(expert_routes.reshape(length, TOP))
    mixing = route_weights.reshape(length, TOP)
    mixed = rms_norm(x_attn, gains[1]).astype(jnp.bfloat16)
    pad_rows = jnp.concatenate([mixed, jnp.zeros((1, D), jnp.bfloat16)], axis=0)
    send_token = jnp.where(slot_pair < length * TOP, slot_pair // TOP, length)
    outgoing = pad_rows[send_token].reshape(shards, local_experts * CAP_EXP, D)
    arrived = lax.all_to_all(outgoing, "ep", split_axis=0, concat_axis=0, tiled=True).reshape(
        shards, local_experts, CAP_EXP, D
    )
    gate_val = jnp.einsum("sjcd,jdf->sjcf", arrived, gate_up, preferred_element_type=jnp.float32)
    gate_part = gate_val[..., :FF]
    up_part = gate_val[..., FF:]
    sigma = jax.nn.sigmoid(gate_part)
    hidden = (gate_part * sigma * up_part).astype(jnp.bfloat16)
    produced = jnp.einsum(
        "sjcf,jfd->sjcd", hidden, down, preferred_element_type=jnp.float32
    ).astype(jnp.bfloat16)
    returned = lax.all_to_all(
        produced.reshape(shards, local_experts * CAP_EXP, D),
        "ep",
        split_axis=0,
        concat_axis=0,
        tiled=True,
    )
    chosen = (
        returned.reshape(EXPERTS * CAP_EXP, D)[pair_slot]
        .reshape(length, TOP, D)
        .astype(jnp.float32)
    )
    x_final = x_attn + jnp.sum(mixing[:, :, None] * chosen, axis=1)
    places = action_positions.reshape(act_count)
    final = rms_norm(x_final, gains[2])
    picked = final[places]
    value_pred = jnp.dot(picked, gains[3], precision=lax.Precision.HIGHEST)
    group_rows = lax.all_gather(picked.astype(jnp.bfloat16), "ep", axis=0, tiled=True)
    logits = jnp.einsum("ad,vd->av", group_rows, table, preferred_element_type=jnp.float32)
    targets = action_tokens.reshape(shards * act_count) - shard_index * vocab_rows
    target_mask = jnp.arange(vocab_rows, dtype=jnp.int32)[None, :] == targets[:, None]
    target_logit = jnp.sum(jnp.where(target_mask, logits, 0.0), axis=1)
    local_peak = jnp.max(logits, axis=1)
    local_mass = jnp.sum(jnp.exp(logits - local_peak[:, None]), axis=1)
    all_peak, all_mass, all_target = combined_all(
        (local_peak, local_mass, target_logit), "ep", combine_stats
    )
    log_norm = all_peak + jnp.log(all_mass)
    logp = all_target - log_norm
    group_adv = advantages.reshape(shards * act_count)
    own_logp = lax.dynamic_slice_in_dim(logp, shard_index * act_count, act_count)
    own_adv = lax.dynamic_slice_in_dim(group_adv, shard_index * act_count, act_count)
    own_targets = value_targets.reshape(act_count)
    local_loss = jnp.sum(-own_adv * own_logp + VALUE_COEF * (value_pred - own_targets) ** 2)
    soft = jnp.exp(logits - log_norm[:, None])
    d_logits = ((group_adv / npos)[:, None] * (soft - target_mask.astype(jnp.float32))).astype(
        jnp.bfloat16
    )
    grad_table = jnp.einsum("av,ad->vd", d_logits, group_rows, preferred_element_type=jnp.float32)
    head_part = jnp.einsum("av,vd->ad", d_logits, table, preferred_element_type=jnp.float32)
    grad_picked = lax.psum_scatter(head_part, "ep", scatter_dimension=0, tiled=True)
    grad_value = 2.0 * VALUE_COEF * (value_pred - own_targets) / npos
    grad_picked = grad_picked + grad_value[:, None] * gains[3][None, :]
    grad_vhead = jnp.dot(grad_value, picked, precision=lax.Precision.HIGHEST)
    grad_final = jnp.zeros((length, D), jnp.float32).at[places].add(grad_picked)
    _, final_back = jax.vjp(rms_norm, x_final, gains[2])
    grad_x_final, grad_gain_two = final_back(grad_final)
    grad_pairs = (
        (mixing[:, :, None] * grad_x_final[:, None, :])
        .reshape(length * TOP, D)
        .astype(jnp.bfloat16)
    )
    grad_pad = jnp.concatenate([grad_pairs, jnp.zeros((1, D), jnp.bfloat16)], axis=0)
    grad_outgoing = grad_pad[slot_pair].reshape(shards, local_experts * CAP_EXP, D)
    grad_arrived = lax.all_to_all(
        grad_outgoing, "ep", split_axis=0, concat_axis=0, tiled=True
    ).reshape(shards, local_experts, CAP_EXP, D)
    grad_down = jnp.einsum(
        "sjcf,sjcd->jfd", hidden, grad_arrived, preferred_element_type=jnp.float32
    )
    grad_hidden = jnp.einsum(
        "sjcd,jfd->sjcf", grad_arrived, down, preferred_element_type=jnp.float32
    )
    grad_gate = grad_hidden * up_part * sigma * (1.0 + gate_part * (1.0 - sigma))
    grad_up = grad_hidden * gate_part * sigma
    grad_gate_val = jnp.concatenate([grad_gate, grad_up], axis=-1).astype(jnp.bfloat16)
    grad_gate_up = jnp.einsum(
        "sjcd,sjcf->jdf", arrived, grad_gate_val, preferred_element_type=jnp.float32
    )
    grad_inputs = jnp.einsum(
        "sjcf,jdf->sjcd", grad_gate_val, gate_up, preferred_element_type=jnp.float32
    ).astype(jnp.bfloat16)
    grad_back = lax.all_to_all(
        grad_inputs.reshape(shards, local_experts * CAP_EXP, D),
        "ep",
        split_axis=0,
        concat_axis=0,
        tiled=True,
    )
    grad_mixed = jnp.sum(
        grad_back.reshape(EXPERTS * CAP_EXP, D)[pair_slot]
        .reshape(length, TOP, D)
        .astype(jnp.float32),
        axis=1,
    )
    _, mixed_back = jax.vjp(rms_norm, x_attn, gains[1])
    grad_norm_in, grad_gain_one = mixed_back(grad_mixed)
    grad_x_attn = grad_x_final + grad_norm_in
    grad_attn_low = grad_x_attn.astype(jnp.bfloat16)
    grad_w_out = jnp.einsum(
        "ti,td->id", attended, grad_attn_low, preferred_element_type=jnp.float32
    )
    grad_attended = jnp.einsum(
        "td,id->ti", grad_attn_low, w_out, preferred_element_type=jnp.float32
    )
    grad_attended = grad_attended.astype(jnp.bfloat16).reshape(length, KV, groups_per, HD)
    probs = jnp.exp(score_block() - log_denom)
    probs_again = probs.astype(jnp.bfloat16)
    grad_values = jnp.einsum(
        "kgts,tkgd->skd", probs_again, grad_attended, preferred_element_type=jnp.float32
    )
    grad_probs = jnp.einsum(
        "tkgd,skd->kgts", grad_attended, values_low, preferred_element_type=jnp.float32
    )
    row_delta = jnp.sum(grad_probs * probs, axis=-1, keepdims=True)
    grad_scores = (probs * (grad_probs - row_delta)).astype(jnp.bfloat16)
    grad_query = (
        jnp.einsum("kgts,skd->tkgd", grad_scores, keys_low, preferred_element_type=jnp.float32)
        * score_scale
    )
    grad_keys = (
        jnp.einsum("kgts,tkgd->skd", grad_scores, query_low, preferred_element_type=jnp.float32)
        * score_scale
    )
    grad_query = (
        rotate_back(grad_query.reshape(length, HEADS, HD), cosine, sine_table)
        .reshape(length, HEADS * HD)
        .astype(jnp.bfloat16)
    )
    grad_keys = rotate_back(grad_keys, cosine, sine_table)
    grad_keyval = (
        jnp.stack([grad_keys, grad_values], axis=1)
        .reshape(length, 2 * KV * HD)
        .astype(jnp.bfloat16)
    )
    grad_w_query = jnp.einsum("td,ti->di", normed, grad_query, preferred_element_type=jnp.float32)
    grad_w_keyval = jnp.einsum("td,ti->di", normed, grad_keyval, preferred_element_type=jnp.float32)
    grad_normed = jnp.einsum(
        "ti,di->td", grad_query, w_query, preferred_element_type=jnp.float32
    ) + jnp.einsum("ti,di->td", grad_keyval, w_keyval, preferred_element_type=jnp.float32)
    _, embed_back = jax.vjp(rms_norm, x_embed, gains[0])
    grad_norm_embed, grad_gain_zero = embed_back(grad_normed)
    grad_rows = (embed_scale * (grad_x_attn + grad_norm_embed)).astype(jnp.bfloat16)
    all_rows = lax.all_gather(grad_rows, "ep", axis=0, tiled=True)
    grad_table = grad_table + jax.ops.segment_sum(
        jnp.where(inside[:, None], all_rows.astype(jnp.float32), 0.0),
        safe_ids,
        num_segments=vocab_rows,
    )
    grad_gains = jnp.stack([grad_gain_zero, grad_gain_one, grad_gain_two, grad_vhead])
    att_grads = lax.psum((grad_w_query, grad_w_keyval, grad_w_out, grad_gains), "ep")
    column_grad = jnp.concatenate(
        [grad_gate_up.reshape(-1), grad_down.reshape(-1), grad_table.reshape(-1)]
        + [piece.reshape(-1) for piece in att_grads]
    ).reshape(blocks, row_width)
    padded_grad = jnp.concatenate([column_grad, jnp.zeros((1, row_width), jnp.float32)], axis=0)
    layout = padded_grad[block_of_row]
    owned = lax.psum_scatter(layout, "grp", scatter_dimension=0, tiled=True)
    own_blocks = lax.dynamic_slice_in_dim(block_of_row, group_index * capacity, capacity)
    filled = own_blocks < blocks
    col_blocks = col_size // row_width
    counted = filled & ((own_blocks < col_blocks) | (shard_index == 0))
    square = jnp.sum(jnp.where(counted[:, None], owned * owned, 0.0))
    square_all, loss_all = lax.psum((square, local_loss), ("grp", "ep"))
    grad_norm = jnp.sqrt(square_all)
    factor = jnp.minimum(1.0, CLIP_BASE / math.sqrt(npos) / grad_norm)
    clipped = factor * owned.reshape(capacity, 1, row_width)
    new_first = BETA_ONE * first_moment + (1.0 - BETA_ONE) * clipped
    new_second = BETA_TWO * second_moment + (1.0 - BETA_TWO) * clipped * clipped
    step_size = (
        new_first
        / (1.0 - BETA_ONE**ADAM_STEP)
        / (jnp.sqrt(new_second / (1.0 - BETA_TWO**ADAM_STEP)) + ADAM_EPS)
    )
    new_master = master_weights - LEARN_RATE * (step_size + WEIGHT_DECAY * master_weights)
    keep_rows = filled.reshape(capacity, 1, 1)
    return (
        loss_all / npos,
        grad_norm,
        jnp.where(keep_rows, new_master, 0.0),
        jnp.where(keep_rows, new_first, 0.0),
        jnp.where(keep_rows, new_second, 0.0),
    )


def solution(mesh):
    placed = (
        P("grp", None, None),
        P("grp", "ep", None, None),
        P("grp", "ep", None, None),
        P("grp", "ep", None),
        P("grp", None, None),
        P("grp", None, None),
        P("grp", "ep", None),
        P(),
        P("grp", "ep", None),
        P("grp", "ep", None),
        P("grp", "ep", None),
    )
    return jax.shard_map(
        on_device,
        mesh=mesh,
        in_specs=placed,
        out_specs=(P(), P(), P("grp", "ep", None), P("grp", "ep", None), P("grp", "ep", None)),
        check_vma=False,
    )
```

profile of v0, /device:TPU:0, one launch (start us, length us, event | category | flops | bytes accessed | tf_op | source)
XLA Modules:
  0.0 4771.7 jit_solution(55169134345315282)
XLA Ops:
  7.2 26.0 convert_element_type.209
  37.1 1066.5 %all-gather.12.cloned.1.call-done = bf16[7688,1,4096]{2,1,0:T(2,128)(2,1)} async-done(((bf16[1922,1,4096]{2,1,0:T(2,128)(2,1)}), bf16[7688,1,4096]{2,1,0:T(2,128)(2,1)}) %all-gather.12.cloned.1.call-update) | async-done | bytes 62980112 | tf_op jit(solution)/shard_map/all_gather | solution.py:136
  1103.6 104.0 %copy.177 = bf16[7688,1,4096]{2,0,1:T(8,128)(2,1)} copy(bf16[7688,1,4096]{2,1,0:T(2,128)(2,1)} %all-gather.12.cloned.1.call-done) | data formatting | bytes 125960192
  1207.5 81.6 %gather_fusion = bf16[3843,4096]{1,0:T(8,128)(2,1)} fusion(bf16[7688,4096]{1,0:T(8,128)(2,1)} %bitcast.297, s32[4096]{0:T(1024)S(1)} %pad_clamp_fusion.1), kind=kCustom, calls=%fused_computation | custom fusion | bytes 62979084 | tf_op jit(solution)/shard_map/gather | solution.py:139
  1300.0 20.5 reshape.453
  1320.5 17.1 gather_fusion.1
  1457.3 105.0 %all-to-all-done = bf16[8,384,1024]{2,1,0:T(8,128)(2,1)} async-done(((bf16[8,384,1024]{2,1,0:T(8,128)(2,1)}), bf16[8,384,1024]{2,1,0:T(8,128)(2,1)}, u32[]{:S(2)}, u32[]{:S(2)}) %all-to-all-start) | async-done | bytes 6291488 | tf_op jit(solution)/shard_map/all_to_all | solution.py:193
  1598.3 138.5 %all-to-all-done.1 = bf16[8,384,1024]{2,1,0:T(8,128)(2,1)} async-done(((bf16[8,384,1024]{2,1,0:T(8,128)(2,1)}), bf16[8,384,1024]{2,1,0:T(8,128)(2,1)}, u32[]{:S(2)}, u32[]{:S(2)}) %all-to-all-start.1) | async-done | bytes 6291488 | tf_op jit(solution)/shard_map/all_to_all | solution.py:204
  1736.8 14.7 gather_fusion.3
  1757.4 14.9 all_gather.28
  1823.1 29.4 reduce-scatter.7.cloned.1.call-done
  1859.3 18.6 gather_fusion.5
  1883.4 19.5 scatter_custom_fusion.1
  1917.5 104.2 %all-to-all-done.2 = bf16[8,384,1024]{2,1,0:T(8,128)(2,1)} async-done(((bf16[8,384,1024]{2,1,0:T(8,128)(2,1)}), bf16[8,384,1024]{2,1,0:T(8,128)(2,1)}, u32[]{:S(2)}, u32[]{:S(2)}) %all-to-all-start.2) | async-done | bytes 6291488 | tf_op jit(solution)/shard_map/all_to_all | solution.py:258
  2059.2 14.6 copy.135
  2104.6 116.2 %all-to-all-done.3 = bf16[8,384,1024]{2,1,0:T(8,128)(2,1)} async-done(((bf16[8,384,1024]{2,1,0:T(8,128)(2,1)}), bf16[8,384,1024]{2,1,0:T(8,128)(2,1)}, u32[]{:S(2)}, u32[]{:S(2)}) %all-to-all-start.3) | async-done | bytes 6291488 | tf_op jit(solution)/shard_map/all_to_all | solution.py:276
  2220.9 15.0 gather_fusion.6
  2270.9 28.6 psum.46
  2300.1 37.0 scatter_custom_fusion.3
  2359.5 196.7 %all-reduce.10.cloned.1.call-done = (f32[1048576]{0:T(1024)}, f32[1048576]{0:T(1024)}, f32[1048576]{0:T(1024)}) async-done(((f32[1048576]{0:T(1024)}, f32[1048576]{0:T(1024)}, f32[1048576]{0:T(1024)}), (f32[1048576]{0:T(1024)}, f32[1048576]{0:T(1024)}, f32[1048576]{0:T(1024)})) %all-reduce.10.cloned.1.call-update) | async-done | bytes 12582928 | tf_op jit(solution)/shard_map/psum | solution.py:344
  2567.4 67.4 %reshape.482 = f32[3843,4096]{1,0:T(8,128)} reshape(f32[15740928]{0:T(1024)} %constant_dynamic-update-slice_fusion) | data formatting | bytes 125927424 | tf_op jit(solution)/shard_map/reshape | solution.py:348
  2634.9 42.8 concatenate.45
  2677.6 351.2 %gather_fusion.7 = f32[7688,4096]{1,0:T(8,128)} fusion(f32[3844,4096]{1,0:T(8,128)} %concatenate.45, s32[8192]{0:T(1024)S(1)} %copy-done.37), kind=kCustom, calls=%fused_computation.7 | custom fusion | bytes 251951136 | tf_op jit(solution)/shard_map/gather | solution.py:350
  3028.8 1276.8 %fusion = f32[2000,4096]{1,0:T(8,128)} fusion(f32[7688,4096]{1,0:T(8,128)} %gather_fusion.7), kind=kCustom, calls=%all-reduce-scatter | all-reduce-scatter fusion | flops 32768000 | bytes 158728704
  4316.5 79.1 %collective-permute-done = f32[234,4096]{1,0:T(8,128)} collective-permute-done((f32[234,4096]{1,0:T(8,128)}, f32[234,4096]{1,0:T(8,128)}, u32[]{:S(2)}, u32[]{:S(2)}) %collective-permute-start) | collective-permute-done | bytes 3833888
  4395.7 85.5 %concatenate.46 = f32[2234,4096]{1,0:T(8,128)} concatenate(f32[234,4096]{1,0:T(8,128)} %collective-permute-done, f32[2000,4096]{1,0:T(8,128)} %fusion), dimensions={0} | concatenate | bytes 73203712
  4481.1 16.5 select_reduce_fusion
  4497.6 41.7 all-reduce.6
  4540.0 82.9 %broadcast_select_fusion = (f32[1922,1,4096]{2,0,1:T(8,128)}, f32[1922,1,4096]{2,0,1:T(8,128)}, f32[1922,1,4096]{2,0,1:T(8,128)}) fusion(pred[1922]{0:T(1024)(128)(4,1)S(1)} %get-tuple-element.236, f32[2234,4096]{1,0:T(8,128)} %concatenate.46, u32[]{:S(6)} %subtract, f32[]{:T(128)S(6)} %min.16, f32[1922,1,4096]{2,1,0:T(1,128)} %param.23, ...), kind=kLoop, calls=%fused_computation.25 | loop fusion | flops 149577728 | bytes 220432272 | tf_op jit(solution)/shard_map/jit(_where)/select_n | solution.py:375
  4622.9 46.3 copy.112
  4669.2 46.3 copy.113
  4715.5 46.3 copy.114
  (333 shorter events, 400.7 us)
Async XLA Ops:
  7.2 1096.4 %all-gather.12.cloned.1.call-start = ((), (), s32[]{:S(2)}) async-start(), calls=%async_computation.9 | async-start | bytes 157450240 | tf_op jit(solution)/shard_map/all_gather | solution.py:136
  33.2 1358.4 %reduce-scatter.5.cloned.1.call-start = ((), (), s32[]{:S(2)}) async-start(), calls=%async_computation.6 | async-start | bytes 4718592 | tf_op jit(solution)/shard_map/reduce_scatter | solution.py:152
  37.0 1170.5 %copy-start.42 = (s32[3843]{0:T(1024)}, s32[3843]{0:T(1024)S(1)}, u32[]{:S(2)}) copy-start(s32[3843]{0:T(1024)S(1)} %compare_select_fusion.3) | copy-start | bytes 46120
  1320.5 17.1 copy-start.47
  1360.9 37.6 copy-start.27
  1360.9 37.6 copy-start.29
  1370.7 11.0 copy-start.5
  1381.7 14.5 copy-start.20
  1387.1 11.5 copy-start.38
  1387.1 17.2 copy-start.40
  1392.9 7.2 copy-start.54
  1404.2 14.2 copy-start.56
  1404.2 352.1 %copy-start.3 = (f32[256,1024]{1,0:T(8,128)}, f32[256,1024]{1,0:T(8,128)S(1)}, u32[]{:S(2)}) copy-start(f32[256,1024]{1,0:T(8,128)S(1)} %get-tuple-element.276) | copy-start | bytes 3145732
  1404.3 14.1 copy-start.49
  1418.4 143.8 %all-to-all-start = ((bf16[8,384,1024]{2,1,0:T(8,128)(2,1)}), bf16[8,384,1024]{2,1,0:T(8,128)(2,1)}, u32[]{:S(2)}, u32[]{:S(2)}) async-start(bf16[8,384,1024]{2,1,0:T(8,128)(2,1)} %bitcast.305), calls=%async_computation.1 | async-start | bytes 12582912 | tf_op jit(solution)/shard_map/all_to_all | solution.py:193
  1592.9 143.9 %all-to-all-start.1 = ((bf16[8,384,1024]{2,1,0:T(8,128)(2,1)}), bf16[8,384,1024]{2,1,0:T(8,128)(2,1)}, u32[]{:S(2)}, u32[]{:S(2)}) async-start(bf16[8,384,1024]{2,1,0:T(8,128)(2,1)} %bitcast.302), calls=%async_computation.2 | async-start | bytes 12582912 | tf_op jit(solution)/shard_map/all_to_all | solution.py:204
  1597.9 254.6 %reduce-scatter.7.cloned.1.call-start = ((), (), s32[]{:S(2)}) async-start(), calls=%async_computation.7 | async-start | bytes 1179648 | tf_op jit(solution)/shard_map/reduce_scatter | solution.py:244
  1779.1 9.6 copy-start.2
  1810.1 11.5 copy-start.61
  1877.9 143.8 %all-to-all-start.2 = ((bf16[8,384,1024]{2,1,0:T(8,128)(2,1)}), bf16[8,384,1024]{2,1,0:T(8,128)(2,1)}, u32[]{:S(2)}, u32[]{:S(2)}) async-start(bf16[8,384,1024]{2,1,0:T(8,128)(2,1)} %bitcast.304), calls=%async_computation.4 | async-start | bytes 12582912 | tf_op jit(solution)/shard_map/all_to_all | solution.py:258
  1903.0 14.6 copy-start.35
  2059.2 14.6 copy-start.14
  2077.2 143.7 %all-to-all-start.3 = ((bf16[8,384,1024]{2,1,0:T(8,128)(2,1)}), bf16[8,384,1024]{2,1,0:T(8,128)(2,1)}, u32[]{:S(2)}, u32[]{:S(2)}) async-start(bf16[8,384,1024]{2,1,0:T(8,128)(2,1)} %bitcast.303), calls=%async_computation.5 | async-start | bytes 12582912 | tf_op jit(solution)/shard_map/all_to_all | solution.py:276
  2081.9 217.8 %all-gather.10.cloned.1.call-start = ((), (), s32[]{:S(2)}) async-start(), calls=%async_computation.8 | async-start | bytes 4718592 | tf_op jit(solution)/shard_map/all_gather | solution.py:337
  2082.0 11.5 copy-start.19
  2220.8 20.7 copy-start.4
  2220.8 20.7 copy-start.41
  2220.9 20.7 copy-start.50
  2253.4 302.8 %all-reduce.10.cloned.1.call-start = ((), (), s32[]{:S(2)}) async-start(), calls=%async_computation.10 | async-start | bytes 25165824 | tf_op jit(solution)/shard_map/psum | solution.py:344
  2634.9 42.8 copy-start.37
  4305.6 8.9 copy-start.62
  4310.1 85.5 %collective-permute-start = (f32[234,4096]{1,0:T(8,128)}, f32[234,4096]{1,0:T(8,128)}, u32[]{:S(2)}, u32[]{:S(2)}) collective-permute-start(f32[234,4096]{1,0:T(8,128)} %slice.198), channel_id=1, source_target_pairs={{0,8},{8,16},{16,24},{1,9},{9,17},{17,25},{2,10},{10,18},{18,26},{... | collective-permute-start | bytes 11501576
  (42 other events, 123.8 us)
Sparse Core Ops, SparseCore 0:
  33.4 1070.1 all-gather.11
  1341.6 49.9 reduce-scatter.4
  1821.5 30.9 reduce-scatter.6
  2253.5 46.2 all-gather.9
  2302.8 253.4 all-reduce.9
where the time goes:
time: 4790 us; the launch traced here: 4770 us
  waiting for transfers between devices  1840 us (38%)
  blocking collectives  1390 us (29%)
  local copies, waits for them, and re-layouts  1170 us (24%)
  other arithmetic  210 us (4%)
  matrix products  114 us (2%)
    unnamed x1, blocking collectives  1280 us
    all_gather x1, waiting for transfers between devices, on_device(): lax.all_gather(master_weights.reshape(capacity, row_width).astype(jnp.bfl...  1070 us
    unnamed x156, local copies, waits for them, and re-layouts  419 us
    gather x1, local copies, waits for them, and re-layouts, on_device(): layout = padded_grad[block_of_row]  351 us
    psum x1, waiting for transfers between devices, on_device(): lax.psum((grad_w_query, grad_w_keyval, grad_w_out, grad_gains), 'ep')  197 us
    all_to_all x1, waiting for transfers between devices, on_device(): lax.all_to_all(produced.reshape(shards, local_experts * CAP_EXP, D), 'ep'...  139 us
    all_to_all x1, waiting for transfers between devices, on_device(): lax.all_to_all(grad_inputs.reshape(shards, local_experts * CAP_EXP, D), '...  116 us
    all_to_all x1, waiting for transfers between devices, on_device(): lax.all_to_all(outgoing, 'ep', split_axis=0, concat_axis=0, tiled=True)  105 us
  transfers between devices with their start and end apart: 10, of which 10 were waited for; matrix products, arithmetic and copies ran while one was open for 5% of the time, Pallas kernels for 0%

commit v1 on v0

--- a/solution.py
+++ b/solution.py
@@ -1,8 +1,11 @@
+import functools
 import math
 
 import jax
 import jax.numpy as jnp
 from jax import lax
+from jax.experimental import pallas as pl
+from jax.experimental.pallas import tpu as pltpu
 from jax.sharding import PartitionSpec as P
 
 D = 1024
@@ -27,6 +30,9 @@
 WEIGHT_DECAY = 0.1
 ROPE_BASE = 10000.0
 MASK_FILL = -1e30
+LANES = 128
+CHUNK = 64
+BATCH = 64
 
 
 def combined_all(value, axis, combine):
@@ -84,6 +90,374 @@
         .set(jnp.arange(pairs, dtype=jnp.int32))
     )
     return (pair_slot, slot_pair)
+
+
+def ring_order(count):
+    side = math.isqrt(count)
+    if side * side != count or side % 2:
+        return list(range(count))
+    path = []
+    for y in range(side):
+        row = range(1, side) if y % 2 == 0 else range(side - 1, 0, -1)
+        path += [y * side + x for x in row]
+    path += [y * side for y in range(side - 1, -1, -1)]
+    return path
+
+
+def cast_kernel(src_ref, out_ref):
+    out_ref[...] = src_ref[...].astype(jnp.bfloat16)
+
+
+def cast_rows(rows, extra):
+    count, sub, _ = rows.shape
+    return pl.pallas_call(
+        cast_kernel,
+        out_shape=jax.ShapeDtypeStruct((count + extra, sub, LANES), jnp.bfloat16),
+        grid=(pl.cdiv(count, BATCH),),
+        in_specs=[pl.BlockSpec((BATCH, sub, LANES), lambda i: (i, 0, 0))],
+        out_specs=pl.BlockSpec((BATCH, sub, LANES), lambda i: (i, 0, 0)),
+        name="cast_rows",
+    )(rows)
+
+
+def fetch_blocks(idx_ref, first_ref, second_ref, buf, sem, step, slot):
+    limit = first_ref.shape[0]
+
+    def body(k, carry):
+        b = idx_ref[step * BATCH + k]
+
+        @pl.when(b < limit)
+        def _():
+            pltpu.make_async_copy(first_ref.at[b], buf.at[slot, k], sem.at[slot]).start()
+
+        @pl.when(b >= limit)
+        def _():
+            pltpu.make_async_copy(second_ref.at[b - limit], buf.at[slot, k], sem.at[slot]).start()
+
+        return carry
+
+    lax.fori_loop(0, BATCH, body, 0, unroll=8)
+
+
+def unpack_kernel(idx_ref, first_ref, second_ref, out_ref, buf, wide, sem):
+    i = pl.program_id(0)
+    slot = lax.rem(i, 2)
+
+    @pl.when(i == 0)
+    def _():
+        fetch_blocks(idx_ref, first_ref, second_ref, buf, sem, 0, 0)
+
+    @pl.when(i + 1 < pl.num_programs(0))
+    def _():
+        fetch_blocks(idx_ref, first_ref, second_ref, buf, sem, i + 1, 1 - slot)
+
+    pltpu.make_async_copy(first_ref.at[pl.ds(0, BATCH)], buf.at[slot], sem.at[slot]).wait()
+    sub = buf.shape[2]
+    per = D // LANES
+    wide[...] = buf[slot].astype(jnp.float32).reshape(BATCH * sub, LANES)
+    for j in range(per):
+        out_ref[:, LANES * j : LANES * (j + 1)] = wide[
+            pl.ds(j, BATCH * sub // per, stride=per), :
+        ].astype(jnp.bfloat16)
+
+
+def pad_index(index):
+    count = index.shape[0]
+    return jnp.pad(index, (0, pl.cdiv(count, BATCH) * BATCH - count)).astype(jnp.int32)
+
+
+def unpack(streams, index):
+    first, second = streams
+    count = index.shape[0]
+    sub = first.shape[1]
+    rows = sub * LANES // D
+    return pl.pallas_call(
+        unpack_kernel,
+        out_shape=jax.ShapeDtypeStruct((count * rows, D), jnp.bfloat16),
+        grid_spec=pltpu.PrefetchScalarGridSpec(
+            num_scalar_prefetch=1,
+            grid=(pl.cdiv(count, BATCH),),
+            in_specs=[pl.BlockSpec(memory_space=pl.ANY), pl.BlockSpec(memory_space=pl.ANY)],
+            out_specs=pl.BlockSpec((BATCH * rows, D), lambda i, idx: (i, 0)),
+            scratch_shapes=[
+                pltpu.VMEM((2, BATCH, sub, LANES), jnp.bfloat16),
+                pltpu.VMEM((BATCH * sub, LANES), jnp.float32),
+                pltpu.SemaphoreType.DMA((2,)),
+            ],
+        ),
+        cost_estimate=pl.CostEstimate(
+            flops=0, bytes_accessed=4 * count * sub * LANES, transcendentals=0
+        ),
+        name="unpack",
+    )(pad_index(index), first, second)
+
+
+def own_kernel(idx_ref, first_ref, second_ref, out_ref, buf, sem):
+    i = pl.program_id(0)
+    slot = lax.rem(i, 2)
+
+    @pl.when(i == 0)
+    def _():
+        fetch_blocks(idx_ref, first_ref, second_ref, buf, sem, 0, 0)
+
+    @pl.when(i + 1 < pl.num_programs(0))
+    def _():
+        fetch_blocks(idx_ref, first_ref, second_ref, buf, sem, i + 1, 1 - slot)
+
+    pltpu.make_async_copy(first_ref.at[pl.ds(0, BATCH)], buf.at[slot], sem.at[slot]).wait()
+    out_ref[...] = buf[slot]
+
+
+def take_blocks(streams, index):
+    first, second = streams
+    count = index.shape[0]
+    sub = first.shape[1]
+    return pl.pallas_call(
+        own_kernel,
+        out_shape=jax.ShapeDtypeStruct((count, sub, LANES), jnp.bfloat16),
+        grid_spec=pltpu.PrefetchScalarGridSpec(
+            num_scalar_prefetch=1,
+            grid=(pl.cdiv(count, BATCH),),
+            in_specs=[pl.BlockSpec(memory_space=pl.ANY), pl.BlockSpec(memory_space=pl.ANY)],
+            out_specs=pl.BlockSpec((BATCH, sub, LANES), lambda i, idx: (i, 0, 0)),
+            scratch_shapes=[
+                pltpu.VMEM((2, BATCH, sub, LANES), jnp.bfloat16),
+                pltpu.SemaphoreType.DMA((2,)),
+            ],
+        ),
+        name="take_blocks",
+    )(pad_index(index), first, second)
+
+
+def pack_kernel(count, keep, idx_ref, src_ref, *refs):
+    first_ref, second_ref, wide, buf, sem = refs[2:] if keep else refs
+    i = pl.program_id(0)
+    steps = pl.num_programs(0)
+    slot = lax.rem(i, 2)
+    limit = first_ref.shape[0]
+    sub = buf.shape[2]
+    per = D // LANES
+    last = count - (pl.cdiv(count, BATCH) - 1) * BATCH
+
+    def drain(which, blocks):
+        pltpu.make_async_copy(
+            buf.at[which, pl.ds(0, blocks)], first_ref.at[pl.ds(0, blocks)], sem.at[which]
+        ).wait()
+
+    @pl.when(i >= 2)
+    def _():
+        drain(slot, BATCH)
+
+    for j in range(per):
+        wide[pl.ds(j, BATCH * sub // per, stride=per), :] = src_ref[
+            :, LANES * j : LANES * (j + 1)
+        ].astype(jnp.float32)
+    buf[slot] = wide[...].reshape(BATCH, sub, LANES).astype(jnp.bfloat16)
+
+    def body(k, carry):
+        b = idx_ref[i * BATCH + k]
+
+        @pl.when(b < limit)
+        def _():
+            pltpu.make_async_copy(buf.at[slot, k], first_ref.at[b], sem.at[slot]).start()
+
+        @pl.when(b >= limit)
+        def _():
+            pltpu.make_async_copy(buf.at[slot, k], second_ref.at[b - limit], sem.at[slot]).start()
+
+        return carry
+
+    @pl.when(i < steps - 1)
+    def _():
+        lax.fori_loop(0, BATCH, body, 0, unroll=8)
+
+    @pl.when(i == steps - 1)
+    def _():
+        lax.fori_loop(0, last, body, 0)
+        drain(slot, last)
+
+        @pl.when(i >= 1)
+        def _():
+            drain(1 - slot, BATCH)
+
+
+def pack(grad, index, size, streams=None):
+    count = index.shape[0]
+    rows = grad.shape[0] // count
+    sub = rows * D // LANES
+    keep = streams is not None
+    shape = jax.ShapeDtypeStruct((size, sub, LANES), jnp.bfloat16)
+    anywhere = pl.BlockSpec(memory_space=pl.ANY)
+    return pl.pallas_call(
+        functools.partial(pack_kernel, count, keep),
+        out_shape=(shape, shape),
+        grid_spec=pltpu.PrefetchScalarGridSpec(
+            num_scalar_prefetch=1,
+            grid=(pl.cdiv(count, BATCH),),
+            in_specs=[pl.BlockSpec((BATCH * rows, D), lambda i, idx: (i, 0))]
+            + ([anywhere, anywhere] if keep else []),
+            out_specs=(anywhere, anywhere),
+            scratch_shapes=[
+                pltpu.VMEM((BATCH * sub, LANES), jnp.float32),
+                pltpu.VMEM((2, BATCH, sub, LANES), jnp.bfloat16),
+                pltpu.SemaphoreType.DMA((2,)),
+            ],
+        ),
+        input_output_aliases={2: 0, 3: 1} if keep else {},
+        cost_estimate=pl.CostEstimate(
+            flops=0, bytes_accessed=6 * count * sub * LANES, transcendentals=0
+        ),
+        name="pack",
+    )(pad_index(index), grad, *(streams if keep else ()))
+
+
+def update_kernel(scal_ref, count_ref, grad_ref, m_ref, f_ref, s_ref, om_ref, of_ref, os_ref):
+    i = pl.program_id(0)
+    rows = grad_ref.shape[0]
+    row = i * rows + lax.broadcasted_iota(jnp.int32, grad_ref.shape, 0)
+    keep = row < count_ref[0]
+    clipped = scal_ref[0] * grad_ref[...].astype(jnp.float32)
+    master = m_ref[...]
+    new_first = BETA_ONE * f_ref[...] + (1.0 - BETA_ONE) * clipped
+    new_second = BETA_TWO * s_ref[...] + (1.0 - BETA_TWO) * clipped * clipped
+    step_size = (
+        new_first
+        / (1.0 - BETA_ONE**ADAM_STEP)
+        / (jnp.sqrt(new_second / (1.0 - BETA_TWO**ADAM_STEP)) + ADAM_EPS)
+    )
+    new_master = master - LEARN_RATE * (step_size + WEIGHT_DECAY * master)
+    om_ref[...] = jnp.where(keep, new_master, 0.0)
+    of_ref[...] = jnp.where(keep, new_first, 0.0)
+    os_ref[...] = jnp.where(keep, new_second, 0.0)
+
+
+def update(factor, valid, grad, master, first, second):
+    count, sub, _ = grad.shape
+    tile = next(t for t in range(64, 0, -1) if count % t == 0)
+    spec = pl.BlockSpec((tile, sub, LANES), lambda i, a, b: (i, 0, 0))
+    shape = jax.ShapeDtypeStruct(grad.shape, jnp.float32)
+    return pl.pallas_call(
+        update_kernel,
+        out_shape=(shape, shape, shape),
+        grid_spec=pltpu.PrefetchScalarGridSpec(
+            num_scalar_prefetch=2,
+            grid=(count // tile,),
+            in_specs=[spec] * 4,
+            out_specs=(spec, spec, spec),
+        ),
+        name="update",
+    )(factor.reshape(1), valid.reshape(1), grad, master, first, second)
+
+
+class Part:
+    def __init__(self, lo, hi, member, before, counts_before, ring_pos, my_pos):
+        groups = member.shape[1]
+        self.lo, self.count, self.groups = lo, hi - lo, groups
+        self.size = (hi - lo) // 2 + groups + (groups + 1) * CHUNK
+        inside = member[lo:hi]
+        self.held = jnp.sum(inside, axis=0)
+        self.base = counts_before
+        rank = jnp.sum((before[lo:hi] - counts_before[None, :]) * inside, axis=1)
+        half = (self.held + 1) // 2
+        halves = (half, self.held - half)
+        self.half = half
+        self.steps = []
+        self.gather_seg, self.scatter_seg, self.lag, self.scatter_lag = [], [], [], []
+        padded_sum = []
+        steps = jnp.zeros((), jnp.int32)
+        slots = jnp.arange(groups, dtype=jnp.int32)
+        for way in (0, 1):
+            wide = jnp.maximum(halves[way], CHUNK)
+            at_ring = jnp.sum(jnp.where(ring_pos[None, :] == slots[:, None], wide[None, :], 0), axis=1)
+            steps = jnp.maximum(steps, jnp.max(jnp.sum(at_ring) - at_ring))
+            turn = 1 if way == 0 else -1
+
+            def starts(origin):
+                gap = ((origin - slots) * turn) % groups
+                earlier = gap[None, :] < gap[:, None]
+                return jnp.sum(jnp.where(earlier, at_ring[None, :], 0), axis=1)
+
+            def by_group(ring_values):
+                return jnp.sum(
+                    jnp.where(ring_pos[:, None] == slots[None, :], ring_values[None, :], 0), axis=1
+                )
+
+            here = jnp.sum(jnp.where(slots == my_pos, at_ring, 0))
+            prev = jnp.sum(jnp.where(slots == (my_pos - turn) % groups, at_ring, 0))
+            self.lag.append(here)
+            self.scatter_lag.append(prev)
+            self.gather_seg.append(by_group(starts(my_pos)))
+            self.scatter_seg.append(by_group(starts((my_pos - turn) % groups)))
+        self.dyn_steps = (steps + CHUNK - 1) // CHUNK
+        self.fixed_steps = int(0.45 * (hi - lo)) // CHUNK
+
+        def place(seg):
+            up = jnp.sum((seg[0])[None, :] * inside, axis=1) + rank
+            down = jnp.sum((seg[1] - half)[None, :] * inside, axis=1) + rank + self.size
+            return jnp.where(rank < jnp.sum(half[None, :] * inside, axis=1), up, down)
+
+        self.gather_place = place(self.gather_seg)
+        self.scatter_place = place(self.scatter_seg)
+
+
+def ring_links(count):
+    order = ring_order(count)
+    up = [(order[k], order[(k + 1) % count]) for k in range(count)]
+    return up, [(b, a) for a, b in up]
+
+
+def pick(vector, index):
+    return jnp.sum(jnp.where(jnp.arange(vector.shape[0]) == index, vector, 0))
+
+
+def run_ring(part, streams, step):
+    for s in range(part.fixed_steps):
+        streams = [step(s, way, streams[way]) for way in (0, 1)]
+
+    def body(s, carry):
+        return tuple(step(s, way, carry[way]) for way in (0, 1))
+
+    return lax.fori_loop(part.fixed_steps, part.dyn_steps, body, tuple(streams))
+
+
+def ring_gather(part, own, group_index):
+    links = ring_links(part.groups)
+    base = pick(part.base, group_index)
+    half = pick(part.half, group_index)
+    streams = [
+        lax.dynamic_slice_in_dim(own, start, part.size) for start in (base, base + half)
+    ]
+
+    def step(s, way, stream):
+        sent = lax.dynamic_slice_in_dim(stream, s * CHUNK, CHUNK)
+        got = lax.ppermute(sent, "grp", links[way])
+        at = jnp.minimum(part.lag[way] + s * CHUNK, part.size - CHUNK)
+        return lax.dynamic_update_slice_in_dim(stream, got, at, 0)
+
+    return run_ring(part, streams, step)
+
+
+def ring_scatter(part, streams):
+    links = ring_links(part.groups)
+
+    def step(s, way, stream):
+        sent = lax.dynamic_slice_in_dim(stream, s * CHUNK, CHUNK)
+        got = lax.ppermute(sent, "grp", links[way])
+        at = jnp.minimum(part.scatter_lag[way] + s * CHUNK, part.size - CHUNK)
+        old = lax.dynamic_slice_in_dim(stream, at, CHUNK)
+        total = (old.astype(jnp.float32) + got.astype(jnp.float32)).astype(jnp.bfloat16)
+        return lax.dynamic_update_slice_in_dim(stream, total, at, 0)
+
+    return run_ring(part, streams, step)
+
+
+def own_index(part, group_index, row, offset):
+    k = row - pick(part.base, group_index)
+    half = pick(part.half, group_index)
+    up = pick(part.scatter_seg[0], group_index) + k
+    down = pick(part.scatter_seg[1], group_index) + k - half + part.size
+    inside = (k >= 0) & (k < pick(part.held, group_index))
+    return inside, jnp.where(k < half, up, down) + offset
 
 
 def combine_stats(earlier, later):
@@ -125,25 +499,38 @@
     query_end = col_size + D * HEADS * HD
     keyval_end = query_end + D * 2 * KV * HD
     out_end = keyval_end + HEADS * HD * D
+    sub = row_width // LANES
+    order = ring_order(groups)
+    ring_pos = jnp.array([order.index(g) for g in range(groups)], jnp.int32)
+    my_pos = pick(ring_pos, group_index)
     member = (owners[:, None] == jnp.arange(groups, dtype=jnp.int32)[None, :]).astype(jnp.int32)
-    ranking = jnp.sum((jnp.cumsum(member, axis=0) - member) * member, axis=1)
-    row_of_block = owners * capacity + ranking
-    block_of_row = (
-        jnp.full((groups * capacity,), blocks, jnp.int32)
-        .at[row_of_block]
-        .set(jnp.arange(blocks, dtype=jnp.int32))
-    )
-    gathered = lax.all_gather(
-        master_weights.reshape(capacity, row_width).astype(jnp.bfloat16), "grp", axis=0, tiled=True
-    )
-    column = gathered[row_of_block].reshape(-1)
-    gate_up = column[:gu_size].reshape(local_experts, D, 2 * FF)
-    down = column[gu_size : gu_size + dn_size].reshape(local_experts, FF, D)
-    table = column[gu_size + dn_size : col_size].reshape(vocab_rows, D)
-    w_query = column[col_size:query_end].reshape(D, HEADS * HD)
-    w_keyval = column[query_end:keyval_end].reshape(D, 2 * KV * HD)
-    w_out = column[keyval_end:out_end].reshape(HEADS * HD, D)
-    gains = column[out_end : out_end + 4 * D].reshape(4, D).astype(jnp.float32)
+    before = jnp.cumsum(member, axis=0) - member
+    marks = [0, (gu_size + dn_size) // row_width, col_size // row_width, blocks]
+    parts = []
+    counts_before = jnp.zeros((groups,), jnp.int32)
+    for lo, hi in zip(marks[:-1], marks[1:]):
+        parts.append(Part(lo, hi, member, before, counts_before, ring_pos, my_pos))
+        counts_before = counts_before + parts[-1].held
+    exp_part, tab_part, att_part = parts
+    master_rows = master_weights.reshape(capacity, sub, LANES)
+    own = cast_rows(master_rows, max(part.size for part in parts))
+    tab_streams = ring_gather(tab_part, own, group_index)
+    own, tab_streams = lax.optimization_barrier((own, tab_streams))
+    table = unpack(tab_streams, tab_part.gather_place)
+    att_streams = ring_gather(att_part, own, group_index)
+    own, att_streams = lax.optimization_barrier((own, att_streams))
+    exp_streams = ring_gather(exp_part, own, group_index)
+    gu_nb = gu_size // row_width
+    gate_up = unpack(exp_streams, exp_part.gather_place[:gu_nb]).reshape(local_experts, D, 2 * FF)
+    down = unpack(exp_streams, exp_part.gather_place[gu_nb:]).reshape(local_experts, FF, D)
+    q_nb = (query_end - col_size) // row_width
+    kv_nb = (keyval_end - col_size) // row_width
+    o_nb = (out_end - col_size) // row_width
+    att_place = att_part.gather_place
+    w_query = unpack(att_streams, att_place[:q_nb])
+    w_keyval = unpack(att_streams, att_place[q_nb:kv_nb])
+    w_out = unpack(att_streams, att_place[kv_nb:o_nb])
+    gains = unpack(att_streams, att_place[o_nb:])[: 4].astype(jnp.float32)
     group_ids = token_ids.reshape(shards * length)
     local_ids = group_ids - shard_index * vocab_rows
     inside = (local_ids >= 0) & (local_ids < vocab_rows)
@@ -342,38 +729,46 @@
     )
     grad_gains = jnp.stack([grad_gain_zero, grad_gain_one, grad_gain_two, grad_vhead])
     att_grads = lax.psum((grad_w_query, grad_w_keyval, grad_w_out, grad_gains), "ep")
-    column_grad = jnp.concatenate(
-        [grad_gate_up.reshape(-1), grad_down.reshape(-1), grad_table.reshape(-1)]
-        + [piece.reshape(-1) for piece in att_grads]
-    ).reshape(blocks, row_width)
-    padded_grad = jnp.concatenate([column_grad, jnp.zeros((1, row_width), jnp.float32)], axis=0)
-    layout = padded_grad[block_of_row]
-    owned = lax.psum_scatter(layout, "grp", scatter_dimension=0, tiled=True)
-    own_blocks = lax.dynamic_slice_in_dim(block_of_row, group_index * capacity, capacity)
-    filled = own_blocks < blocks
-    col_blocks = col_size // row_width
-    counted = filled & ((own_blocks < col_blocks) | (shard_index == 0))
-    square = jnp.sum(jnp.where(counted[:, None], owned * owned, 0.0))
+    att_rows = jnp.concatenate([piece.reshape(-1, D) for piece in att_grads], axis=0)
+    exp_sums = pack(grad_gate_up.reshape(-1, D), exp_part.scatter_place[:gu_nb], exp_part.size)
+    exp_sums = pack(
+        grad_down.reshape(-1, D), exp_part.scatter_place[gu_nb:], exp_part.size, exp_sums
+    )
+    exp_sums = ring_scatter(exp_part, exp_sums)
+    tab_sums = ring_scatter(tab_part, pack(grad_table, tab_part.scatter_place, tab_part.size))
+    att_sums = ring_scatter(att_part, pack(att_rows, att_part.scatter_place, att_part.size))
+    row = jnp.arange(capacity, dtype=jnp.int32)
+    valid = pick(counts_before, group_index)
+    filled = row < valid
+    own_col = pick(att_part.base, group_index)
+    pieces = []
+    for part, sums in ((exp_part, exp_sums), (tab_part, tab_sums), (att_part, att_sums)):
+        pieces.append((own_index(part, group_index, row, 0), sums))
+    place = jnp.zeros((capacity,), jnp.int32)
+    offset = 0
+    ups = jnp.concatenate([s[0] for _, s in pieces], axis=0)
+    downs = jnp.concatenate([s[1] for _, s in pieces], axis=0)
+    whole = ups.shape[0]
+    for part, ((inside_part, at), sums) in zip((exp_part, tab_part, att_part), pieces):
+        at = jnp.where(at < part.size, at + offset, at - part.size + offset + whole)
+        place = jnp.where(inside_part, at, place)
+        offset += part.size
+    owned = take_blocks((ups, downs), place)
+    counted = (filled & ((row < own_col) | (shard_index == 0))).reshape(capacity, 1, 1)
+    wide_owned = owned.astype(jnp.float32)
+    square = jnp.sum(jnp.where(counted, wide_owned * wide_owned, 0.0))
     square_all, loss_all = lax.psum((square, local_loss), ("grp", "ep"))
     grad_norm = jnp.sqrt(square_all)
     factor = jnp.minimum(1.0, CLIP_BASE / math.sqrt(npos) / grad_norm)
-    clipped = factor * owned.reshape(capacity, 1, row_width)
-    new_first = BETA_ONE * first_moment + (1.0 - BETA_ONE) * clipped
-    new_second = BETA_TWO * second_moment + (1.0 - BETA_TWO) * clipped * clipped
-    step_size = (
-        new_first
-        / (1.0 - BETA_ONE**ADAM_STEP)
-        / (jnp.sqrt(new_second / (1.0 - BETA_TWO**ADAM_STEP)) + ADAM_EPS)
-    )
-    new_master = master_weights - LEARN_RATE * (step_size + WEIGHT_DECAY * master_weights)
-    keep_rows = filled.reshape(capacity, 1, 1)
-    return (
-        loss_all / npos,
-        grad_norm,
-        jnp.where(keep_rows, new_master, 0.0),
-        jnp.where(keep_rows, new_first, 0.0),
-        jnp.where(keep_rows, new_second, 0.0),
-    )
+    outs = update(
+        factor,
+        valid,
+        owned,
+        master_rows,
+        first_moment.reshape(capacity, sub, LANES),
+        second_moment.reshape(capacity, sub, LANES),
+    )
+    return (loss_all / npos, grad_norm) + tuple(o.reshape(master_weights.shape) for o in outs)
 
 
 def solution(mesh):

time: 4790 us -> 2240 us (0.47)
  waiting for transfers between devices: 1840 us -> 625 us
  blocking collectives: 1390 us -> 256 us
  local copies, waits for them, and re-layouts: 1170 us -> 331 us
  Pallas kernels: 0 us -> 309 us
  starting transfers between devices: 24 us -> 144 us
  other arithmetic: 210 us -> 319 us
  between operations: 19.8 us -> 97.5 us
    unnamed x1 -> x0, blocking collectives: 1280 us -> none
    all_gather x1 -> x0, waiting for transfers between devices: 1070 us -> none  [on_device(): lax.all_gather(master_weights.reshape(capacity, row_width).astype(jnp.bfl...]
    gather x2 -> x0, local copies, waits for them, and re-layouts: 433 us -> none  [the longest x1 351 us: on_device(): layout = padded_grad[block_of_row]]
    unnamed x156 -> x172, local copies, waits for them, and re-layouts: 419 us -> 12.6 us
    pallas_call x0 -> x14, Pallas kernels: none -> 309 us  [the longest x1 80.5 us: update(): pl.pallas_call(update_kernel, out_shape=(shape, shape, shape), grid_spec=...]
    ppermute x0 -> x116, waiting for transfers between devices: none -> 259 us  [step(): got = lax.ppermute(sent, 'grp', links[way])]
    dynamic_slice x0 -> x116, local copies, waits for them, and re-layouts: none -> 161 us  [the longest x113 130 us: step(): sent = lax.dynamic_slice_in_dim(stream, s * CHUNK, CHUNK)]
    all_to_all x0 -> x1, blocking collectives: none -> 144 us  [on_device(): lax.all_to_all(grad_outgoing, 'ep', split_axis=0, concat_axis=0, tiled=True)]
  transfers between devices with their start and end apart: 10 -> 123, of which waited for: 10 -> 75; matrix products, arithmetic and copies ran while one was open for 5% -> 21% of each run, Pallas kernels for 0% -> 5%
where the time goes in v1:
time: 2240 us; the launch traced here: 2220 us
  waiting for transfers between devices  625 us (28%)
  local copies, waits for them, and re-layouts  331 us (15%)
  other arithmetic  319 us (14%)
  Pallas kernels  309 us (14%)
  blocking collectives  256 us (11%)
  starting transfers between devices  144 us (6%)
  matrix products  129 us (6%)
  between operations  97.5 us (4%)
    ppermute x116, waiting for transfers between devices, step(): got = lax.ppermute(sent, 'grp', links[way])  259 us
    all_to_all x1, blocking collectives, on_device(): lax.all_to_all(grad_outgoing, 'ep', split_axis=0, concat_axis=0, tiled=True)  144 us
    all_to_all x1, waiting for transfers between devices, on_device(): lax.all_to_all(produced.reshape(shards, local_experts * CAP_EXP, D), 'ep'...  138 us
    all_to_all x1, waiting for transfers between devices, on_device(): lax.all_to_all(grad_inputs.reshape(shards, local_experts * CAP_EXP, D), '...  137 us
    dynamic_slice x113, local copies, waits for them, and re-layouts, step(): sent = lax.dynamic_slice_in_dim(stream, s * CHUNK, CHUNK)  130 us
    ppermute x116, starting transfers between devices, step(): got = lax.ppermute(sent, 'grp', links[way])  129 us
    dynamic_update_slice x58, other arithmetic, step(): return lax.dynamic_update_slice_in_dim(stream, total, at, 0)  117 us
    pallas_call x1, Pallas kernels, update(): pl.pallas_call(update_kernel, out_shape=(shape, shape, shape), grid_spec=...  80.5 us
  transfers between devices with their start and end apart: 123, of which 75 were waited for; matrix products, arithmetic and copies ran while one was open for 21% of the time, Pallas kernels for 5%

profile of v1, /device:TPU:0, one launch (start us, length us, event | category | flops | bytes accessed | tf_op | source)
XLA Modules:
  0.0 2221.4 jit_solution(15999362770523851041)
XLA Ops:
  14.3 27.5 %cast_rows.1 = bf16[3015,32,128]{2,1,0:T(8,128)(2,1)} custom-call(f32[1922,32,128]{2,1,0:T(8,128)} %bitcast.258), custom_call_target="tpu_custom_call" | custom-call | tf_op jit(solution)/shard_map/cast_rows/pallas_call | solution.py:113
  200.2 31.8 %while.91 = (s32[]{:T(128)}, bf16[1093,32,128]{2,1,0:T(8,128)(2,1)}, bf16[1093,32,128]{2,1,0:T(8,128)(2,1)}, s32[]{:T(128)}, s32[]{:T(128)}, /*index=5*/s32[]{:T...) while((s32[]{:T(128)}, bf16[1093,32,128]{2,1,0:T(8,128)(2,1)}, ...), condition=%wide.region_24.25_spmd, body=%wide.region_23.24_spmd.sunk | while | flops 16 | bytes 8388975 | solution.py:420
  232.0 23.2 %unpack.7 = bf16[6152,1024]{1,0:T(8,128)(2,1)} custom-call(s32[1600]{0:T(1024)} %pad.26.idx_ref, bf16[1093,32,128]{2,1,0:T(8,128)(2,1)} %get-tuple-element.406.first_ref, bf16[1093,32,128]{2,1,0:T(8,128)(2,1)} %get-tuple-element.407.second_ref), custom_call_target="tpu_custom_call" | custom-call | bytes 25198592 | tf_op jit(solution)/shard_map/unpack/pallas_call | solution.py:174
  255.2 17.1 gather_fusion
  375.3 13.9 while.92
  422.6 14.0 gather_fusion.1
  611.3 14.4 unpack.13
  625.7 13.9 fusion.24
  661.9 138.3 %all-to-all-done.1 = bf16[8,384,1024]{2,1,0:T(8,128)(2,1)} async-done(((bf16[8,384,1024]{2,1,0:T(8,128)(2,1)}), bf16[8,384,1024]{2,1,0:T(8,128)(2,1)}, u32[]{:S(2)}, u32[]{:S(2)}) %all-to-all-start.1) | async-done | bytes 6291488 | tf_op jit(solution)/shard_map/all_to_all | solution.py:591
  800.3 14.5 gather_fusion.2
  822.9 14.9 all_gather.24
  891.2 28.6 %reduce-scatter.5.cloned.1.call-done = f32[32,1024]{1,0:T(8,128)} async-done(((f32[256,1024]{1,0:T(8,128)}), f32[32,1024]{1,0:T(8,128)}) %reduce-scatter.5.cloned.1.call-update) | async-done | bytes 131088 | tf_op jit(solution)/shard_map/reduce_scatter | solution.py:631
  929.7 18.6 gather_fusion.4
  948.2 144.3 %all_to_all.20 = bf16[8,384,1024]{2,1,0:T(8,128)(2,1)} all-to-all(bf16[8,384,1024]{2,1,0:T(8,128)(2,1)} %bitcast.265), channel_id=1, replica_groups=mesh['grp'=4,'ep'=8] {'ep'}, dimensions={0} | all-to-all | bytes 12582912 | tf_op jit(solution)/shard_map/all_to_all | solution.py:645
  1130.5 137.2 %all-to-all-done.3 = bf16[8,384,1024]{2,1,0:T(8,128)(2,1)} async-done(((bf16[8,384,1024]{2,1,0:T(8,128)(2,1)}), bf16[8,384,1024]{2,1,0:T(8,128)(2,1)}, u32[]{:S(2)}, u32[]{:S(2)}) %all-to-all-start.3) | async-done | bytes 6291488 | tf_op jit(solution)/shard_map/all_to_all | solution.py:663
  1267.7 14.5 gather_fusion.5
  1303.3 14.1 fusion.16
  1317.4 18.1 pack.4
  1509.4 36.1 %scatter_custom_fusion.2.src_ref = f32[6152,1024]{1,0:T(8,128)} fusion(f32[6152,1024]{1,0:T(8,128)} %fusion.184, s32[2048]{0:T(1024)S(1)} %bitcast.331, bf16[2048,1024]{1,0:T(8,128)(2,1)} %all-gather.8.cloned.1.call-done, f32[]{:T(128)} %constant.392.clone.1, pred[2048]{0:T(1024)(128)(4,1)S(1)} %copy-done.52), kind=kCustom, calls=%fused_computation.52 | custom fusion | flops 6291456 | bytes 29395456 | tf_op jit(solution)/shard_map/scatter-add | solution.py:725
  1545.5 26.3 %pack.6 = (bf16[1093,32,128]{2,1,0:T(8,128)(2,1)}, bf16[1093,32,128]{2,1,0:T(8,128)(2,1)}) custom-call(s32[1600]{0:T(1024)} %pad.29.idx_ref, f32[6152,1024]{1,0:T(8,128)} %scatter_custom_fusion.2.src_ref), custom_call_target="tpu_custom_call" | custom-call | bytes 37797888 | tf_op jit(solution)/shard_map/pack/pallas_call | solution.py:291
  1645.3 27.6 %psum.46 = f32[4,1024]{1,0:T(4,128)S(1)} all-reduce(f32[4,1024]{1,0:T(4,128)S(1)} %pad_maximum_fusion.9), channel_id=1, replica_groups=mesh['grp'=4,'ep'=8] {'ep'}, use_global_device_ids=true, to_apply=%region_132.133 | all-reduce | flops 4096 | bytes 32768 | tf_op jit(solution)/shard_map/psum | solution.py:731
  1681.1 62.0 %all-reduce.12.cloned.1.call-done = (f32[1024,1024]{1,0:T(8,128)}, f32[1024,1024]{1,0:T(8,128)}, f32[1024,1024]{1,0:T(8,128)}) async-done(((f32[1024,1024]{1,0:T(8,128)}, f32[1024,1024]{1,0:T(8,128)}, f32[1024,1024]{1,0:T(8,128)}), (f32[1024,1024]{1,0:T(8,128)}, f32[1024,1024]{1,0:T(8,128)}, f32[1024,1024]{1,0:T(8,128)})) %all-reduce.12.cloned.1.call-update) | async-done | bytes 12582928 | tf_op jit(solution)/shard_map/psum | solution.py:731
  1752.5 14.2 pack.7
  1888.5 17.6 while.95
  1906.1 16.4 while.97
  1922.5 30.3 %while.96 = (s32[]{:T(128)}, bf16[1093,32,128]{2,1,0:T(8,128)(2,1)}, bf16[1093,32,128]{2,1,0:T(8,128)(2,1)}, s32[]{:T(128)}, s32[]{:T(128)}, /*index=5*/s32[]{:T...) while((s32[]{:T(128)}, bf16[1093,32,128]{2,1,0:T(8,128)(2,1)}, ...), condition=%wide.region_123.124_spmd, body=%wide.region_122.123_spmd.sunk | while | flops 2097168 | bytes 9437551 | solution.py:420
  1952.8 27.8 %pad_maximum_fusion.1.second_ref = bf16[2893,32,128]{2,1,0:T(8,128)(2,1)} fusion(bf16[708,32,128]{2,1,0:T(8,128)(2,1)} %get-tuple-element.432, bf16[1093,32,128]{2,1,0:T(8,128)(2,1)} %get-tuple-element.431, bf16[1092,32,128]{2,1,0:T(8,128)(2,1)} %get-tuple-element.430), kind=kLoop, calls=%fused_computation.45 | loop fusion | flops 23699456 | bytes 47398912 | tf_op jit(solution)/shard_map/concatenate | solution.py:750
  1980.6 27.8 %pad_maximum_fusion.first_ref = bf16[2893,32,128]{2,1,0:T(8,128)(2,1)} fusion(bf16[708,32,128]{2,1,0:T(8,128)(2,1)} %get-tuple-element.429, bf16[1093,32,128]{2,1,0:T(8,128)(2,1)} %get-tuple-element.426, bf16[1092,32,128]{2,1,0:T(8,128)(2,1)} %get-tuple-element.423), kind=kLoop, calls=%fused_computation.44 | loop fusion | flops 23699456 | bytes 47398912 | tf_op jit(solution)/shard_map/concatenate | solution.py:749
  2008.4 66.3 %take_blocks.1.grad_ref = bf16[1922,32,128]{2,1,0:T(8,128)(2,1)} custom-call(s32[1984]{0:T(1024)} %pad.28.idx_ref, bf16[2893,32,128]{2,1,0:T(8,128)(2,1)} %pad_maximum_fusion.first_ref, bf16[2893,32,128]{2,1,0:T(8,128)(2,1)} %pad_maximum_fusion.1.second_ref), custom_call_target="tpu_custom_call" | custom-call | tf_op jit(solution)/shard_map/take_blocks/pallas_call | solution.py:215
  2074.7 15.6 select_reduce_fusion
  2090.3 40.3 %all-reduce.8 = (f32[]{:T(128)}, f32[]{:T(128)}) all-reduce(f32[]{:T(128)} %get-tuple-element.699, f32[]{:T(128)} %select_reduce_fusion), channel_id=1, replica_groups=mesh['grp'=4,'ep'=8] {'grp','ep'}, use_global_device_ids=true, to_apply=%region_82.83 | all-reduce | flops 2 | bytes 16 | tf_op jit(solution)/shard_map/psum | solution.py:760
  2131.9 80.5 %update.1 = (f32[1922,32,128]{2,1,0:T(8,128)}, f32[1922,32,128]{2,1,0:T(8,128)}, f32[1922,32,128]{2,1,0:T(8,128)}) custom-call(f32[1]{0:T(128)} %bitcast.92.scal_ref, s32[1]{0:T(128)} %bitcast.93.count_ref, bf16[1922,32,128]{2,1,0:T(8,128)(2,1)} %take_blocks.1.grad_ref, f32[1922,32,128]{2,1,0:T(8,128)} %bitcast.259, f32[1922,32,128]{2,1,0:T(8,128)} %bitcast.260, ...), custom_call_target="tpu_custom_call" | custom-call | tf_op jit(solution)/shard_map/update/pallas_call | solution.py:339
  (851 shorter events, 1049.1 us)
Async XLA Ops:
  7.2 402.1 %reduce-scatter.3.cloned.1.call-start = ((), (), s32[]{:S(2)}) async-start(), calls=%async_computation.6 | async-start | bytes 4718592 | tf_op jit(solution)/shard_map/reduce_scatter | solution.py:539
  43.8 24.3 %collective-permute-start.22 = (bf16[64,32,128]{2,1,0:T(8,128)(2,1)S(1)}, bf16[64,32,128]{2,1,0:T(8,128)(2,1)S(1)}, u32[]{:S(2)}, u32[]{:S(2)}) collective-permute-start(bf16[64,32,128]{2,1,0:T(8,128)(2,1)S(1)} %get-tuple-element.669), channel_id=1, source_target_pairs={{24,8},{16,24},{0,16},{8,0},{25,9},{17,25},{1,17},{9,1},{26,10},{1... | collective-permute-start | bytes 1572872 | tf_op jit(solution)/shard_map/ppermute | solution.py:433
  46.8 25.2 %collective-permute-start.12 = (bf16[64,32,128]{2,1,0:T(8,128)(2,1)S(1)}, bf16[64,32,128]{2,1,0:T(8,128)(2,1)S(1)}, u32[]{:S(2)}, u32[]{:S(2)}) collective-permute-start(bf16[64,32,128]{2,1,0:T(8,128)(2,1)S(1)} %get-tuple-element.670), channel_id=1, source_target_pairs={{8,24},{24,16},{16,0},{0,8},{9,25},{25,17},{17,1},{1,9},{10,26},{2... | collective-permute-start | bytes 1572872 | tf_op jit(solution)/shard_map/ppermute | solution.py:433
  85.3 20.7 collective-permute-start.24
  89.0 20.7 collective-permute-start.14
  280.8 30.9 %collective-permute-start.37 = (bf16[64,32,128]{2,1,0:T(8,128)(2,1)S(1)}, bf16[64,32,128]{2,1,0:T(8,128)(2,1)S(1)}, u32[]{:S(2)}, u32[]{:S(2)}) collective-permute-start(bf16[64,32,128]{2,1,0:T(8,128)(2,1)S(1)} %get-tuple-element.665), channel_id=1, source_target_pairs={{24,8},{16,24},{0,16},{8,0},{25,9},{17,25},{1,17},{9,1},{26,10},{1... | collective-permute-start | bytes 1572872 | tf_op jit(solution)/shard_map/ppermute | solution.py:433
  327.9 21.1 collective-permute-start.39
  436.6 189.1 %all-to-all-start = ((bf16[8,384,1024]{2,1,0:T(8,128)(2,1)}), bf16[8,384,1024]{2,1,0:T(8,128)(2,1)}, u32[]{:S(2)}, u32[]{:S(2)}) async-start(bf16[8,384,1024]{2,1,0:T(8,128)(2,1)} %bitcast.264), calls=%async_computation.1 | async-start | bytes 12582912 | tf_op jit(solution)/shard_map/all_to_all | solution.py:580
  656.4 143.8 %all-to-all-start.1 = ((bf16[8,384,1024]{2,1,0:T(8,128)(2,1)}), bf16[8,384,1024]{2,1,0:T(8,128)(2,1)}, u32[]{:S(2)}, u32[]{:S(2)}) async-start(bf16[8,384,1024]{2,1,0:T(8,128)(2,1)} %bitcast.262), calls=%async_computation.2 | async-start | bytes 12582912 | tf_op jit(solution)/shard_map/all_to_all | solution.py:591
  661.3 258.4 %reduce-scatter.5.cloned.1.call-start = ((), (), s32[]{:S(2)}) async-start(), calls=%async_computation.7 | async-start | bytes 1179648 | tf_op jit(solution)/shard_map/reduce_scatter | solution.py:631
  1123.9 143.8 %all-to-all-start.3 = ((bf16[8,384,1024]{2,1,0:T(8,128)(2,1)}), bf16[8,384,1024]{2,1,0:T(8,128)(2,1)}, u32[]{:S(2)}, u32[]{:S(2)}) async-start(bf16[8,384,1024]{2,1,0:T(8,128)(2,1)} %bitcast.263), calls=%async_computation.5 | async-start | bytes 12582912 | tf_op jit(solution)/shard_map/all_to_all | solution.py:663
  1128.8 380.6 %all-gather.8.cloned.1.call-start = ((), (), s32[]{:S(2)}) async-start(), calls=%async_computation.8 | async-start | bytes 4718592 | tf_op jit(solution)/shard_map/all_gather | solution.py:724
  1303.1 440.0 %all-reduce.12.cloned.1.call-start = ((), (), s32[]{:S(2)}) async-start(), calls=%async_computation.9 | async-start | bytes 25165824 | tf_op jit(solution)/shard_map/psum | solution.py:731
  1423.6 44.7 %collective-permute-start.76 = (bf16[64,32,128]{2,1,0:T(8,128)(2,1)}, bf16[64,32,128]{2,1,0:T(8,128)(2,1)}, u32[]{:S(2)}, u32[]{:S(2)}) collective-permute-start(bf16[64,32,128]{2,1,0:T(8,128)(2,1)} %dynamic_slice.772), channel_id=1, source_target_pairs={{24,8},{16,24},{0,16},{8,0},{25,9},{17,25},{1,17},{9,1},{26,10},{1... | collective-permute-start | bytes 1572872 | tf_op jit(solution)/shard_map/ppermute | solution.py:445
  1429.1 44.7 %collective-permute-start.66 = (bf16[64,32,128]{2,1,0:T(8,128)(2,1)}, bf16[64,32,128]{2,1,0:T(8,128)(2,1)}, u32[]{:S(2)}, u32[]{:S(2)}) collective-permute-start(bf16[64,32,128]{2,1,0:T(8,128)(2,1)} %dynamic_slice.763), channel_id=1, source_target_pairs={{8,24},{24,16},{16,0},{0,8},{9,25},{25,17},{17,1},{1,9},{10,26},{2... | collective-permute-start | bytes 1572872 | tf_op jit(solution)/shard_map/ppermute | solution.py:445
  1490.3 86.0 %collective-permute-start.78 = (bf16[64,32,128]{2,1,0:T(8,128)(2,1)S(1)}, bf16[64,32,128]{2,1,0:T(8,128)(2,1)S(1)}, u32[]{:S(2)}, u32[]{:S(2)}) collective-permute-start(bf16[64,32,128]{2,1,0:T(8,128)(2,1)S(1)} %dynamic_slice.774), channel_id=1, source_target_pairs={{24,8},{16,24},{0,16},{8,0},{25,9},{17,25},{1,17},{9,1},{26,10},{1... | collective-permute-start | bytes 1572872 | tf_op jit(solution)/shard_map/ppermute | solution.py:445
  1495.2 85.7 %collective-permute-start.68 = (bf16[64,32,128]{2,1,0:T(8,128)(2,1)S(1)}, bf16[64,32,128]{2,1,0:T(8,128)(2,1)S(1)}, u32[]{:S(2)}, u32[]{:S(2)}) collective-permute-start(bf16[64,32,128]{2,1,0:T(8,128)(2,1)S(1)} %dynamic_slice.765), channel_id=1, source_target_pairs={{8,24},{24,16},{16,0},{0,8},{9,25},{25,17},{17,1},{1,9},{10,26},{2... | collective-permute-start | bytes 1572872 | tf_op jit(solution)/shard_map/ppermute | solution.py:445
  1579.4 19.6 collective-permute-start.79
  1584.0 19.6 collective-permute-start.69
  1595.4 19.4 collective-permute-start.83
  1606.6 19.5 collective-permute-start.70
  1617.9 19.8 collective-permute-start.84
  1629.2 140.1 %collective-permute-start.71 = (bf16[64,32,128]{2,1,0:T(8,128)(2,1)S(1)}, bf16[64,32,128]{2,1,0:T(8,128)(2,1)S(1)}, u32[]{:S(2)}, u32[]{:S(2)}) collective-permute-start(bf16[64,32,128]{2,1,0:T(8,128)(2,1)S(1)} %dynamic_slice.768), channel_id=1, source_target_pairs={{8,24},{24,16},{16,0},{0,8},{9,25},{25,17},{17,1},{1,9},{10,26},{2... | collective-permute-start | bytes 1572872 | tf_op jit(solution)/shard_map/ppermute | solution.py:445
  1635.7 37.1 %collective-permute-start.95 = (bf16[64,32,128]{2,1,0:T(8,128)(2,1)S(1)}, bf16[64,32,128]{2,1,0:T(8,128)(2,1)S(1)}, u32[]{:S(2)}, u32[]{:S(2)}) collective-permute-start(bf16[64,32,128]{2,1,0:T(8,128)(2,1)S(1)} %dynamic_slice.789), channel_id=1, source_target_pairs={{24,8},{16,24},{0,16},{8,0},{25,9},{17,25},{1,17},{9,1},{26,10},{1... | collective-permute-start | bytes 1572872 | tf_op jit(solution)/shard_map/ppermute | solution.py:445
  1640.8 36.8 %collective-permute-start.85 = (bf16[64,32,128]{2,1,0:T(8,128)(2,1)S(1)}, bf16[64,32,128]{2,1,0:T(8,128)(2,1)S(1)}, u32[]{:S(2)}, u32[]{:S(2)}) collective-permute-start(bf16[64,32,128]{2,1,0:T(8,128)(2,1)S(1)} %dynamic_slice.780), channel_id=1, source_target_pairs={{8,24},{24,16},{16,0},{0,8},{9,25},{25,17},{17,1},{1,9},{10,26},{2... | collective-permute-start | bytes 1572872 | tf_op jit(solution)/shard_map/ppermute | solution.py:445
  1676.0 97.0 %collective-permute-start.96 = (bf16[64,32,128]{2,1,0:T(8,128)(2,1)S(1)}, bf16[64,32,128]{2,1,0:T(8,128)(2,1)S(1)}, u32[]{:S(2)}, u32[]{:S(2)}) collective-permute-start(bf16[64,32,128]{2,1,0:T(8,128)(2,1)S(1)} %dynamic_slice.790), channel_id=1, source_target_pairs={{24,8},{16,24},{0,16},{8,0},{25,9},{17,25},{1,17},{9,1},{26,10},{1... | collective-permute-start | bytes 1572872 | tf_op jit(solution)/shard_map/ppermute | solution.py:445
  1680.7 96.9 %collective-permute-start.86 = (bf16[64,32,128]{2,1,0:T(8,128)(2,1)S(1)}, bf16[64,32,128]{2,1,0:T(8,128)(2,1)S(1)}, u32[]{:S(2)}, u32[]{:S(2)}) collective-permute-start(bf16[64,32,128]{2,1,0:T(8,128)(2,1)S(1)} %dynamic_slice.781), channel_id=1, source_target_pairs={{8,24},{24,16},{16,0},{0,8},{9,25},{25,17},{17,1},{1,9},{10,26},{2... | collective-permute-start | bytes 1572872 | tf_op jit(solution)/shard_map/ppermute | solution.py:445
  1801.5 19.4 collective-permute-start.88
  1808.2 19.4 collective-permute-start.109
  1812.8 19.4 collective-permute-start.104
  1819.4 19.4 collective-permute-start.99
  1846.4 19.4 collective-permute-start.90
  (173 other events, 3731.3 us)
Sparse Core Ops, SparseCore 0:
  276.3 49.7 reduce-scatter.2
  889.7 30.0 reduce-scatter.4
  1303.2 45.7 all-gather.7
  1487.1 255.9 all-reduce.11

commit v2 on v1

--- a/solution.py
+++ b/solution.py
@@ -31,18 +31,8 @@
 ROPE_BASE = 10000.0
 MASK_FILL = -1e30
 LANES = 128
-CHUNK = 64
+CHUNK = 128
 BATCH = 64
-
-
-def combined_all(value, axis, combine):
-    everything = jax.tree.map(lambda part: lax.all_gather(part, axis), value)
-    initial = jax.tree.map(lambda part: part[0], everything)
-
-    def turn(k, so_far):
-        return combine(so_far, jax.tree.map(lambda part: part[k], everything))
-
-    return lax.fori_loop(1, lax.axis_size(axis), turn, initial)
 
 
 def rms_norm(values, gain_row):
@@ -74,22 +64,6 @@
     return jnp.concatenate(
         [front * cosine + behind * sine_table, behind * cosine - front * sine_table], axis=-1
     )
-
-
-def slot_tables(routes):
-    flat_routes = routes.reshape(-1)
-    pairs = flat_routes.shape[0]
-    member = (flat_routes[:, None] == jnp.arange(EXPERTS, dtype=jnp.int32)[None, :]).astype(
-        jnp.int32
-    )
-    ranking = jnp.sum((jnp.cumsum(member, axis=0) - member) * member, axis=1)
-    pair_slot = flat_routes * CAP_EXP + ranking
-    slot_pair = (
-        jnp.full((EXPERTS * CAP_EXP,), pairs, jnp.int32)
-        .at[pair_slot]
-        .set(jnp.arange(pairs, dtype=jnp.int32))
-    )
-    return (pair_slot, slot_pair)
 
 
 def ring_order(count):
@@ -192,33 +166,51 @@
     )(pad_index(index), first, second)
 
 
-def own_kernel(idx_ref, first_ref, second_ref, out_ref, buf, sem):
+def own_kernel(limits, idx_ref, *refs):
+    sources = refs[: len(limits)]
+    out_ref, buf, sem = refs[len(limits) :]
     i = pl.program_id(0)
     slot = lax.rem(i, 2)
 
+    def fetch(step, which):
+        def body(k, carry):
+            b = idx_ref[step * BATCH + k]
+            start = 0
+            for source, limit in zip(sources, limits):
+
+                @pl.when((b >= start) & (b < start + limit))
+                def _(source=source, start=start):
+                    pltpu.make_async_copy(
+                        source.at[b - start], buf.at[which, k], sem.at[which]
+                    ).start()
+
+                start += limit
+            return carry
+
+        lax.fori_loop(0, BATCH, body, 0, unroll=8)
+
     @pl.when(i == 0)
     def _():
-        fetch_blocks(idx_ref, first_ref, second_ref, buf, sem, 0, 0)
+        fetch(0, 0)
 
     @pl.when(i + 1 < pl.num_programs(0))
     def _():
-        fetch_blocks(idx_ref, first_ref, second_ref, buf, sem, i + 1, 1 - slot)
-
-    pltpu.make_async_copy(first_ref.at[pl.ds(0, BATCH)], buf.at[slot], sem.at[slot]).wait()
+        fetch(i + 1, 1 - slot)
+
+    pltpu.make_async_copy(sources[0].at[pl.ds(0, BATCH)], buf.at[slot], sem.at[slot]).wait()
     out_ref[...] = buf[slot]
 
 
 def take_blocks(streams, index):
-    first, second = streams
     count = index.shape[0]
-    sub = first.shape[1]
+    sub = streams[0].shape[1]
     return pl.pallas_call(
-        own_kernel,
+        functools.partial(own_kernel, tuple(s.shape[0] for s in streams)),
         out_shape=jax.ShapeDtypeStruct((count, sub, LANES), jnp.bfloat16),
         grid_spec=pltpu.PrefetchScalarGridSpec(
             num_scalar_prefetch=1,
             grid=(pl.cdiv(count, BATCH),),
-            in_specs=[pl.BlockSpec(memory_space=pl.ANY), pl.BlockSpec(memory_space=pl.ANY)],
+            in_specs=[pl.BlockSpec(memory_space=pl.ANY)] * len(streams),
             out_specs=pl.BlockSpec((BATCH, sub, LANES), lambda i, idx: (i, 0, 0)),
             scratch_shapes=[
                 pltpu.VMEM((2, BATCH, sub, LANES), jnp.bfloat16),
@@ -226,7 +218,7 @@
             ],
         ),
         name="take_blocks",
-    )(pad_index(index), first, second)
+    )(pad_index(index), *streams)
 
 
 def pack_kernel(count, keep, idx_ref, src_ref, *refs):
@@ -460,10 +452,16 @@
     return inside, jnp.where(k < half, up, down) + offset
 
 
-def combine_stats(earlier, later):
-    top_score = jnp.maximum(earlier[0], later[0])
-    mass = earlier[1] * jnp.exp(earlier[0] - top_score) + later[1] * jnp.exp(later[0] - top_score)
-    return (top_score, mass, earlier[2] + later[2])
+def sum_everywhere(values):
+    values = jnp.zeros((8, LANES), jnp.float32).at[0, : values.shape[0]].set(values)
+    for axis in ("ep", "grp"):
+        size = lax.axis_size(axis)
+        step = 1
+        while step < size:
+            pairs = [(k, k ^ step) for k in range(size)]
+            values = values + lax.ppermute(values, axis, pairs)
+            step *= 2
+    return values[0, 0], values[0, 1]
 
 
 def on_device(
@@ -539,17 +537,66 @@
     x_embed = embed_scale * lax.psum_scatter(found, "ep", scatter_dimension=0, tiled=True).astype(
         jnp.float32
     )
+    places = action_positions.reshape(act_count)
     cosine, sine_table = rope_tables(length)
     score_scale = HD ** (-0.5)
+    rows = length
+    slots = CAP_EXP
     causal = jnp.arange(length)[:, None] >= jnp.arange(length)[None, :]
+    sum_type = jnp.bfloat16
+
+    def take(values):
+        return values
+
+    def put(values):
+        return values
+
+    cosine_q, sine_q = take(cosine), take(sine_table)
+    routing = jnp.concatenate(
+        [
+            take(expert_routes.reshape(length, TOP)).astype(jnp.float32),
+            take(route_weights.reshape(length, TOP)),
+        ],
+        axis=1,
+    )
+    routing = lax.all_gather(routing, "ep", axis=0)
+    local_ids_exp = shard_index * local_experts + jnp.arange(local_experts, dtype=jnp.int32)
+    named = routing[:, :, None, :TOP] == local_ids_exp[None, None, :, None].astype(jnp.float32)
+    routed = jnp.sum(named.astype(jnp.float32), axis=3)
+    pair_weight = jnp.sum(jnp.where(named, routing[:, :, None, TOP:], 0.0), axis=3)
+    earlier_row = (jnp.arange(rows)[:, None] < jnp.arange(rows)[None, :]).astype(jnp.bfloat16)
+    slot_of = jnp.einsum(
+        "pt,spj->sjt",
+        earlier_row,
+        routed.astype(jnp.bfloat16),
+        preferred_element_type=jnp.float32,
+    )
+    slot_of = jnp.where(jnp.swapaxes(routed, 1, 2) > 0.0, slot_of, -1.0)
+    held = slot_of[:, :, None, :] == jnp.arange(slots, dtype=jnp.float32)[None, None, :, None]
+    dealt = held.astype(jnp.bfloat16)
+    slot_weight = jnp.sum(
+        jnp.where(held, jnp.swapaxes(pair_weight, 1, 2)[:, :, None, :], 0.0), axis=3
+    )[..., None]
+
+    def to_experts(values):
+        return jnp.einsum("sjcp,spd->sjcd", dealt, values, preferred_element_type=jnp.float32)
+
+    def from_experts(values):
+        partial = jnp.einsum(
+            "sjcp,sjcd->spd", dealt, values, preferred_element_type=jnp.float32
+        ).astype(sum_type)
+        return lax.psum_scatter(
+            partial.reshape(shards * rows, D), "ep", scatter_dimension=0, tiled=True
+        ).astype(jnp.float32)
+
     normed = rms_norm(x_embed, gains[0]).astype(jnp.bfloat16)
-    query = jnp.dot(normed, w_query, preferred_element_type=jnp.float32).reshape(length, HEADS, HD)
+    normed_q = take(normed)
+    query = jnp.dot(normed_q, w_query, preferred_element_type=jnp.float32).reshape(rows, HEADS, HD)
     keyval = jnp.dot(normed, w_keyval, preferred_element_type=jnp.float32).reshape(
         length, 2, KV, HD
     )
-    query_low = (
-        rotate(query, cosine, sine_table).astype(jnp.bfloat16).reshape(length, KV, groups_per, HD)
-    )
+    query_low = rotate(query, cosine_q, sine_q).astype(jnp.bfloat16)
+    query_low = query_low.reshape(rows, KV, groups_per, HD)
     keys_low = rotate(keyval[:, 0], cosine, sine_table).astype(jnp.bfloat16)
     values_low = keyval[:, 1].astype(jnp.bfloat16)
 
@@ -569,17 +616,11 @@
     attended = jnp.einsum(
         "kgts,skd->tkgd", probs_low, values_low, preferred_element_type=jnp.float32
     )
-    attended = attended.reshape(length, HEADS * HD).astype(jnp.bfloat16)
-    x_attn = x_embed + jnp.dot(attended, w_out, preferred_element_type=jnp.float32)
-    pair_slot, slot_pair = slot_tables(expert_routes.reshape(length, TOP))
-    mixing = route_weights.reshape(length, TOP)
+    attended = attended.reshape(rows, HEADS * HD).astype(jnp.bfloat16)
+    x_attn = take(x_embed) + jnp.dot(attended, w_out, preferred_element_type=jnp.float32)
     mixed = rms_norm(x_attn, gains[1]).astype(jnp.bfloat16)
-    pad_rows = jnp.concatenate([mixed, jnp.zeros((1, D), jnp.bfloat16)], axis=0)
-    send_token = jnp.where(slot_pair < length * TOP, slot_pair // TOP, length)
-    outgoing = pad_rows[send_token].reshape(shards, local_experts * CAP_EXP, D)
-    arrived = lax.all_to_all(outgoing, "ep", split_axis=0, concat_axis=0, tiled=True).reshape(
-        shards, local_experts, CAP_EXP, D
-    )
+    mixed_all = lax.all_gather(mixed, "ep", axis=0)
+    arrived = to_experts(mixed_all).astype(jnp.bfloat16)
     gate_val = jnp.einsum("sjcd,jdf->sjcf", arrived, gate_up, preferred_element_type=jnp.float32)
     gate_part = gate_val[..., :FF]
     up_part = gate_val[..., FF:]
@@ -588,20 +629,8 @@
     produced = jnp.einsum(
         "sjcf,jfd->sjcd", hidden, down, preferred_element_type=jnp.float32
     ).astype(jnp.bfloat16)
-    returned = lax.all_to_all(
-        produced.reshape(shards, local_experts * CAP_EXP, D),
-        "ep",
-        split_axis=0,
-        concat_axis=0,
-        tiled=True,
-    )
-    chosen = (
-        returned.reshape(EXPERTS * CAP_EXP, D)[pair_slot]
-        .reshape(length, TOP, D)
-        .astype(jnp.float32)
-    )
-    x_final = x_attn + jnp.sum(mixing[:, :, None] * chosen, axis=1)
-    places = action_positions.reshape(act_count)
+    weighted = (slot_weight * produced.astype(jnp.float32)).astype(jnp.bfloat16)
+    x_final = x_attn + from_experts(weighted)
     final = rms_norm(x_final, gains[2])
     picked = final[places]
     value_pred = jnp.dot(picked, gains[3], precision=lax.Precision.HIGHEST)
@@ -612,9 +641,10 @@
     target_logit = jnp.sum(jnp.where(target_mask, logits, 0.0), axis=1)
     local_peak = jnp.max(logits, axis=1)
     local_mass = jnp.sum(jnp.exp(logits - local_peak[:, None]), axis=1)
-    all_peak, all_mass, all_target = combined_all(
-        (local_peak, local_mass, target_logit), "ep", combine_stats
-    )
+    stats = lax.all_gather(jnp.stack([local_peak, local_mass, target_logit]), "ep", axis=0)
+    all_peak = jnp.max(stats[:, 0], axis=0)
+    all_mass = jnp.sum(stats[:, 1] * jnp.exp(stats[:, 0] - all_peak[None, :]), axis=0)
+    all_target = jnp.sum(stats[:, 2], axis=0)
     log_norm = all_peak + jnp.log(all_mass)
     logp = all_target - log_norm
     group_adv = advantages.reshape(shards * act_count)
@@ -635,16 +665,8 @@
     grad_final = jnp.zeros((length, D), jnp.float32).at[places].add(grad_picked)
     _, final_back = jax.vjp(rms_norm, x_final, gains[2])
     grad_x_final, grad_gain_two = final_back(grad_final)
-    grad_pairs = (
-        (mixing[:, :, None] * grad_x_final[:, None, :])
-        .reshape(length * TOP, D)
-        .astype(jnp.bfloat16)
-    )
-    grad_pad = jnp.concatenate([grad_pairs, jnp.zeros((1, D), jnp.bfloat16)], axis=0)
-    grad_outgoing = grad_pad[slot_pair].reshape(shards, local_experts * CAP_EXP, D)
-    grad_arrived = lax.all_to_all(
-        grad_outgoing, "ep", split_axis=0, concat_axis=0, tiled=True
-    ).reshape(shards, local_experts, CAP_EXP, D)
+    grad_final_all = lax.all_gather(grad_x_final.astype(jnp.bfloat16), "ep", axis=0)
+    grad_arrived = (slot_weight * to_experts(grad_final_all)).astype(jnp.bfloat16)
     grad_down = jnp.einsum(
         "sjcf,sjcd->jfd", hidden, grad_arrived, preferred_element_type=jnp.float32
     )
@@ -660,30 +682,15 @@
     grad_inputs = jnp.einsum(
         "sjcf,jdf->sjcd", grad_gate_val, gate_up, preferred_element_type=jnp.float32
     ).astype(jnp.bfloat16)
-    grad_back = lax.all_to_all(
-        grad_inputs.reshape(shards, local_experts * CAP_EXP, D),
-        "ep",
-        split_axis=0,
-        concat_axis=0,
-        tiled=True,
-    )
-    grad_mixed = jnp.sum(
-        grad_back.reshape(EXPERTS * CAP_EXP, D)[pair_slot]
-        .reshape(length, TOP, D)
-        .astype(jnp.float32),
-        axis=1,
-    )
+    grad_mixed = from_experts(grad_inputs)
     _, mixed_back = jax.vjp(rms_norm, x_attn, gains[1])
     grad_norm_in, grad_gain_one = mixed_back(grad_mixed)
     grad_x_attn = grad_x_final + grad_norm_in
     grad_attn_low = grad_x_attn.astype(jnp.bfloat16)
-    grad_w_out = jnp.einsum(
-        "ti,td->id", attended, grad_attn_low, preferred_element_type=jnp.float32
-    )
     grad_attended = jnp.einsum(
         "td,id->ti", grad_attn_low, w_out, preferred_element_type=jnp.float32
     )
-    grad_attended = grad_attended.astype(jnp.bfloat16).reshape(length, KV, groups_per, HD)
+    grad_attended = grad_attended.astype(jnp.bfloat16).reshape(rows, KV, groups_per, HD)
     probs = jnp.exp(score_block() - log_denom)
     probs_again = probs.astype(jnp.bfloat16)
     grad_values = jnp.einsum(
@@ -703,8 +710,8 @@
         * score_scale
     )
     grad_query = (
-        rotate_back(grad_query.reshape(length, HEADS, HD), cosine, sine_table)
-        .reshape(length, HEADS * HD)
+        rotate_back(grad_query.reshape(rows, HEADS, HD), cosine_q, sine_q)
+        .reshape(rows, HEADS * HD)
         .astype(jnp.bfloat16)
     )
     grad_keys = rotate_back(grad_keys, cosine, sine_table)
@@ -713,22 +720,41 @@
         .reshape(length, 2 * KV * HD)
         .astype(jnp.bfloat16)
     )
-    grad_w_query = jnp.einsum("td,ti->di", normed, grad_query, preferred_element_type=jnp.float32)
-    grad_w_keyval = jnp.einsum("td,ti->di", normed, grad_keyval, preferred_element_type=jnp.float32)
-    grad_normed = jnp.einsum(
-        "ti,di->td", grad_query, w_query, preferred_element_type=jnp.float32
+    grad_normed = put(
+        jnp.einsum("ti,di->td", grad_query, w_query, preferred_element_type=jnp.float32)
     ) + jnp.einsum("ti,di->td", grad_keyval, w_keyval, preferred_element_type=jnp.float32)
     _, embed_back = jax.vjp(rms_norm, x_embed, gains[0])
     grad_norm_embed, grad_gain_zero = embed_back(grad_normed)
-    grad_rows = (embed_scale * (grad_x_attn + grad_norm_embed)).astype(jnp.bfloat16)
-    all_rows = lax.all_gather(grad_rows, "ep", axis=0, tiled=True)
+    grad_rows = (embed_scale * (put(grad_x_attn) + grad_norm_embed)).astype(jnp.bfloat16)
+    grad_gains = jnp.stack([grad_gain_zero, grad_gain_one, grad_gain_two, grad_vhead])
+    gains_high = grad_gains.astype(jnp.bfloat16)
+    gains_low = (grad_gains - gains_high.astype(jnp.float32)).astype(jnp.bfloat16)
+    ahead = lax.all_gather(jnp.concatenate([attended, normed_q, normed], axis=0), "ep", axis=0)
+    behind = lax.all_gather(
+        jnp.concatenate(
+            [grad_attn_low, grad_query, grad_keyval, grad_rows, gains_high, gains_low], axis=0
+        ),
+        "ep",
+        axis=0,
+    )
+
+    def outer(ins, outs):
+        return jnp.einsum("sti,sto->io", ins, outs, preferred_element_type=jnp.float32)
+
+    grad_w_out = outer(ahead[:, :rows], behind[:, :rows])
+    grad_w_query = outer(ahead[:, rows : 2 * rows], behind[:, rows : 2 * rows])
+    grad_w_keyval = outer(ahead[:, 2 * rows :], behind[:, 2 * rows : 2 * rows + length])
+    all_rows = behind[:, 2 * rows + length : 2 * (rows + length)].reshape(shards * length, D)
+    grad_gains = jnp.sum(
+        behind[:, 2 * (rows + length) :].astype(jnp.float32).reshape(shards, 2, 4, D),
+        axis=(0, 1),
+    )
+    att_grads = (grad_w_query, grad_w_keyval, grad_w_out, grad_gains)
     grad_table = grad_table + jax.ops.segment_sum(
         jnp.where(inside[:, None], all_rows.astype(jnp.float32), 0.0),
         safe_ids,
         num_segments=vocab_rows,
     )
-    grad_gains = jnp.stack([grad_gain_zero, grad_gain_one, grad_gain_two, grad_vhead])
-    att_grads = lax.psum((grad_w_query, grad_w_keyval, grad_w_out, grad_gains), "ep")
     att_rows = jnp.concatenate([piece.reshape(-1, D) for piece in att_grads], axis=0)
     exp_sums = pack(grad_gate_up.reshape(-1, D), exp_part.scatter_place[:gu_nb], exp_part.size)
     exp_sums = pack(
@@ -741,23 +767,17 @@
     valid = pick(counts_before, group_index)
     filled = row < valid
     own_col = pick(att_part.base, group_index)
-    pieces = []
-    for part, sums in ((exp_part, exp_sums), (tab_part, tab_sums), (att_part, att_sums)):
-        pieces.append((own_index(part, group_index, row, 0), sums))
     place = jnp.zeros((capacity,), jnp.int32)
     offset = 0
-    ups = jnp.concatenate([s[0] for _, s in pieces], axis=0)
-    downs = jnp.concatenate([s[1] for _, s in pieces], axis=0)
-    whole = ups.shape[0]
-    for part, ((inside_part, at), sums) in zip((exp_part, tab_part, att_part), pieces):
-        at = jnp.where(at < part.size, at + offset, at - part.size + offset + whole)
+    for part in (exp_part, tab_part, att_part):
+        inside_part, at = own_index(part, group_index, row, offset)
         place = jnp.where(inside_part, at, place)
-        offset += part.size
-    owned = take_blocks((ups, downs), place)
+        offset += 2 * part.size
+    owned = take_blocks((*exp_sums, *tab_sums, *att_sums), place)
     counted = (filled & ((row < own_col) | (shard_index == 0))).reshape(capacity, 1, 1)
     wide_owned = owned.astype(jnp.float32)
     square = jnp.sum(jnp.where(counted, wide_owned * wide_owned, 0.0))
-    square_all, loss_all = lax.psum((square, local_loss), ("grp", "ep"))
+    square_all, loss_all = sum_everywhere(jnp.stack([square, local_loss]))
     grad_norm = jnp.sqrt(square_all)
     factor = jnp.minimum(1.0, CLIP_BASE / math.sqrt(npos) / grad_norm)
     outs = update(

time: 2240 us -> 1780 us (0.79)
  blocking collectives: 256 us -> 43.2 us
  other arithmetic: 319 us -> 212 us
  local copies, waits for them, and re-layouts: 331 us -> 232 us
  starting transfers between devices: 144 us -> 71.1 us
  between operations: 97.5 us -> 63.8 us
  matrix products: 129 us -> 160 us
  waiting for transfers between devices: 625 us -> 651 us
    all_to_all x3 -> x0, waiting for transfers between devices: 276 us -> none  [the longest x1 138 us: on_device(): lax.all_to_all(produced.reshape(shards, local_experts * CAP_EXP, D), 'ep'...]
    all_to_all x1 -> x0, blocking collectives: 144 us -> none  [on_device(): lax.all_to_all(grad_outgoing, 'ep', split_axis=0, concat_axis=0, tiled=True)]
    all_gather x1 -> x4, waiting for transfers between devices: 0.01 us -> 131 us  [the longest x1 85.9 us: on_device(): lax.all_gather(jnp.concatenate([attended, normed_q, normed], axis=0), 'ep...]
    ppermute x116 -> x64, waiting for transfers between devices: 259 us -> 376 us  [step(): got = lax.ppermute(sent, 'grp', links[way])]
    reduce_scatter x0 -> x2, waiting for transfers between devices: none -> 97.9 us  [from_experts(): lax.psum_scatter(partial.reshape(shards * rows, D), 'ep', scatter_dimensi...]
    psum x2 -> x0, blocking collectives: 67.9 us -> none  [the longest x1 40.3 us: on_device(): square_all, loss_all = lax.psum((square, local_loss), ('grp', 'ep'))]
    psum x1 -> x0, waiting for transfers between devices: 62 us -> none  [on_device(): lax.psum((grad_w_query, grad_w_keyval, grad_w_out, grad_gains), 'ep')]
    gather x4 -> x0, local copies, waits for them, and re-layouts: 61.6 us -> none  [the longest x1 18.6 us: on_device(): grad_pad[slot_pair].reshape(shards, local_experts * CAP_EXP, D)]
  transfers between devices with their start and end apart: 123 -> 77, of which waited for: 75 -> 46; matrix products, arithmetic and copies ran while one was open for 21% -> 22% of each run, Pallas kernels for 5% -> 6%
where the time goes in v2:
time: 1780 us; the launch traced here: 1750 us
  waiting for transfers between devices  651 us (37%)
  Pallas kernels  310 us (17%)
  local copies, waits for them, and re-layouts  232 us (13%)
  other arithmetic  212 us (12%)
  matrix products  160 us (9%)
  starting transfers between devices  71.1 us (4%)
  between operations  63.8 us (4%)
  blocking collectives  43.2 us (2%)
    ppermute x64, waiting for transfers between devices, step(): got = lax.ppermute(sent, 'grp', links[way])  376 us
    dynamic_slice x61, local copies, waits for them, and re-layouts, step(): sent = lax.dynamic_slice_in_dim(stream, s * CHUNK, CHUNK)  101 us
    reduce_scatter x2, waiting for transfers between devices, from_experts(): lax.psum_scatter(partial.reshape(shards * rows, D), 'ep', scatter_dimensi...  97.9 us
    all_gather x1, waiting for transfers between devices, on_device(): lax.all_gather(jnp.concatenate([attended, normed_q, normed], axis=0), 'ep...  85.9 us
    dynamic_update_slice x32, other arithmetic, step(): return lax.dynamic_update_slice_in_dim(stream, total, at, 0)  82.2 us
    pallas_call x1, Pallas kernels, update(): pl.pallas_call(update_kernel, out_shape=(shape, shape, shape), grid_spec=...  80.5 us
    ppermute x64, starting transfers between devices, step(): got = lax.ppermute(sent, 'grp', links[way])  69.5 us
    pallas_call x4, Pallas kernels, pack(): pl.pallas_call(functools.partial(pack_kernel, count, keep), out_shape=(sh...  68.6 us
  transfers between devices with their start and end apart: 77, of which 46 were waited for; matrix products, arithmetic and copies ran while one was open for 22% of the time, Pallas kernels for 6%

profile of v2, /device:TPU:0, one launch (start us, length us, event | category | flops | bytes accessed | tf_op | source)
XLA Modules:
  0.0 1754.3 jit_solution(8388718082178886998)
XLA Ops:
  13.5 27.5 %cast_rows.1 = bf16[3335,32,128]{2,1,0:T(8,128)(2,1)} custom-call(f32[1922,32,128]{2,1,0:T(8,128)} %bitcast.263), custom_call_target="tpu_custom_call" | custom-call | tf_op jit(solution)/shard_map/cast_rows/pallas_call | solution.py:87
  48.0 17.3 constant_dynamic-slice_fusion.20
  112.3 16.4 collective-permute-done.19
  138.0 16.0 collective-permute-done.20
  183.7 26.5 %while.73 = (s32[]{:T(128)}, bf16[1413,32,128]{2,1,0:T(8,128)(2,1)}, bf16[1413,32,128]{2,1,0:T(8,128)(2,1)}, s32[]{:T(128)}, s32[]{:T(128)}, /*index=5*/s32[]{:T...) while((s32[]{:T(128)}, bf16[1413,32,128]{2,1,0:T(8,128)(2,1)}, ...), condition=%wide.region_55.56_spmd, body=%wide.region_54.55_spmd.sunk | while | flops 16 | bytes 16777584 | solution.py:412
  190.6 16.1 collective-permute-done.1
  210.2 23.1 %unpack.8 = bf16[6152,1024]{1,0:T(8,128)(2,1)} custom-call(s32[1600]{0:T(1024)} %pad.30.idx_ref, bf16[1413,32,128]{2,1,0:T(8,128)(2,1)} %get-tuple-element.246.first_ref, bf16[1413,32,128]{2,1,0:T(8,128)(2,1)} %get-tuple-element.247.second_ref), custom_call_target="tpu_custom_call" | custom-call | bytes 25198592 | tf_op jit(solution)/shard_map/unpack/pallas_call | solution.py:148
  233.3 17.1 gather_fusion
  311.8 46.8 %while.74 = (s32[]{:T(128)}, bf16[1028,32,128]{2,1,0:T(8,128)(2,1)}, bf16[1028,32,128]{2,1,0:T(8,128)(2,1)}, s32[]{:T(128)}, s32[]{:T(128)}, /*index=5*/s32[]{:T...) while((s32[]{:T(128)}, bf16[1028,32,128]{2,1,0:T(8,128)(2,1)}, ...), condition=%wide.region_63.64_spmd, body=%wide.region_62.63_spmd.sunk | while | flops 16 | bytes 16777584 | solution.py:412
  510.2 31.3 %while.75 = (s32[]{:T(128)}, bf16[1412,32,128]{2,1,0:T(8,128)(2,1)}, bf16[1412,32,128]{2,1,0:T(8,128)(2,1)}, s32[]{:T(128)}, s32[]{:T(128)}, /*index=5*/s32[]{:T...) while((s32[]{:T(128)}, bf16[1412,32,128]{2,1,0:T(8,128)(2,1)}, ...), condition=%wide.region_71.72_spmd, body=%wide.region_70.71_spmd.sunk | while | flops 16 | bytes 16777584 | solution.py:412
  517.3 21.0 %collective-permute-done.5 = bf16[128,32,128]{2,1,0:T(8,128)(2,1)} collective-permute-done((bf16[128,32,128]{2,1,0:T(8,128)(2,1)}, bf16[128,32,128]{2,1,0:T(8,128)(2,1)}, u32[]{:S(2)}, u32[]{:S(2)}) %collective-permute-start.5) | collective-permute-done | bytes 1048608 | tf_op jit(solution)/shard_map/while/body/ppermute | solution.py:425
  602.7 49.7 %reduce-scatter.7.cloned.1.call-done = bf16[256,1024]{1,0:T(8,128)(2,1)} async-done(((bf16[2048,1024]{1,0:T(8,128)(2,1)}), bf16[256,1024]{1,0:T(8,128)(2,1)}) %reduce-scatter.7.cloned.1.call-update) | async-done | bytes 524304 | tf_op jit(solution)/shard_map/reduce_scatter | solution.py:588
  700.0 30.3 %reduce-scatter.9.cloned.1.call-done = f32[32,1024]{1,0:T(8,128)} async-done(((f32[256,1024]{1,0:T(8,128)}), f32[32,1024]{1,0:T(8,128)}) %reduce-scatter.9.cloned.1.call-update) | async-done | bytes 131088 | tf_op jit(solution)/shard_map/reduce_scatter | solution.py:661
  733.4 45.1 %all-gather.14.cloned.1.call-done = bf16[2048,1024]{1,0:T(8,128)(2,1)} async-done(((bf16[256,1024]{1,0:T(8,128)(2,1)}), bf16[2048,1024]{1,0:T(8,128)(2,1)}) %all-gather.14.cloned.1.call-update) | async-done | bytes 4194320 | tf_op jit(solution)/shard_map/all_gather | solution.py:668
  817.1 48.2 %reduce-scatter.11.cloned.1.call-done = bf16[256,1024]{1,0:T(8,128)(2,1)} async-done(((bf16[2048,1024]{1,0:T(8,128)(2,1)}), bf16[256,1024]{1,0:T(8,128)(2,1)}) %reduce-scatter.11.cloned.1.call-update) | async-done | bytes 524304 | tf_op jit(solution)/shard_map/reduce_scatter | solution.py:588
  918.5 18.2 %pack.4 = (bf16[1412,32,128]{2,1,0:T(8,128)(2,1)}, bf16[1412,32,128]{2,1,0:T(8,128)(2,1)}) custom-call(s32[1024]{0:T(1024)} %slice.252.idx_ref, f32[4096,1024]{1,0:T(8,128)} %bitcast.270), custom_call_target="tpu_custom_call" | custom-call | bytes 25165824 | tf_op jit(solution)/shard_map/pack/pallas_call | solution.py:283
  961.8 18.7 %collective-permute-done.41 = bf16[128,32,128]{2,1,0:T(8,128)(2,1)S(1)} collective-permute-done((bf16[128,32,128]{2,1,0:T(8,128)(2,1)}, bf16[128,32,128]{2,1,0:T(8,128)(2,1)S(1)}, u32[]{:S(2)}, u32[]{:S(2)}) %collective-permute-start.41) | collective-permute-done | bytes 1048608 | tf_op jit(solution)/shard_map/ppermute | solution.py:437
  1081.9 85.9 %all-gather.18.cloned.1.call-done = bf16[6144,1024]{1,0:T(8,128)(2,1)} async-done(((bf16[768,1024]{1,0:T(8,128)(2,1)}), bf16[6144,1024]{1,0:T(8,128)(2,1)}) %all-gather.18.cloned.1.call-update) | async-done | bytes 12582928 | tf_op jit(solution)/shard_map/all_gather | solution.py:732
  1177.9 35.9 %scatter_custom_fusion.1.src_ref = f32[6152,1024]{1,0:T(8,128)} fusion(f32[6152,1024]{1,0:T(8,128)} %fusion.199, s32[2048]{0:T(1024)S(1)} %bitcast.330, bf16[2048,1024]{1,0:T(8,128)(2,1)} %bitcast.269, f32[]{:T(128)} %constant.347.clone.1, pred[2048]{0:T(1024)(128)(4,1)S(1)} %copy-done.54), kind=kCustom, calls=%fused_computation.40 | custom fusion | flops 6291456 | bytes 29395456 | tf_op jit(solution)/shard_map/scatter-add | solution.py:753
  1213.7 26.0 %pack.6 = (bf16[1413,32,128]{2,1,0:T(8,128)(2,1)}, bf16[1413,32,128]{2,1,0:T(8,128)(2,1)}) custom-call(s32[1600]{0:T(1024)} %pad.32.idx_ref, f32[6152,1024]{1,0:T(8,128)} %scatter_custom_fusion.1.src_ref), custom_call_target="tpu_custom_call" | custom-call | bytes 37797888 | tf_op jit(solution)/shard_map/pack/pallas_call | solution.py:283
  1252.0 15.7 collective-permute-done.51
  1388.0 18.1 %collective-permute-done.40 = bf16[128,32,128]{2,1,0:T(8,128)(2,1)S(1)} collective-permute-done((bf16[128,32,128]{2,1,0:T(8,128)(2,1)S(1)}, bf16[128,32,128]{2,1,0:T(8,128)(2,1)S(1)}, u32[]{:S(2)}, u32[]{:S(2)}) %collective-permute-start.40) | collective-permute-done | bytes 1048608 | tf_op jit(solution)/shard_map/ppermute | solution.py:437
  1411.1 17.5 collective-permute-done.57
  1450.2 28.6 %while.76 = (s32[]{:T(128)}, bf16[1412,32,128]{2,1,0:T(8,128)(2,1)}, bf16[1412,32,128]{2,1,0:T(8,128)(2,1)}, s32[]{:T(128)}, s32[]{:T(128)}, /*index=5*/s32[]{:T...) while((s32[]{:T(128)}, bf16[1412,32,128]{2,1,0:T(8,128)(2,1)}, ...), condition=%wide.region_109.110_spmd, body=%wide.region_108.109_spmd.sunk | while | flops 4194320 | bytes 18874736 | solution.py:412
  1456.2 17.4 collective-permute-done.7
  1478.8 54.7 %while.78 = (s32[]{:T(128)}, bf16[1028,32,128]{2,1,0:T(8,128)(2,1)}, bf16[1028,32,128]{2,1,0:T(8,128)(2,1)}, s32[]{:T(128)}, s32[]{:T(128)}, /*index=5*/s32[]{:T...) while((s32[]{:T(128)}, bf16[1028,32,128]{2,1,0:T(8,128)(2,1)}, ...), condition=%wide.region_131.132_spmd, body=%wide.region_130.131_spmd.sunk | while | flops 4194320 | bytes 18874736 | solution.py:412
  1484.8 16.5 collective-permute-done.11
  1512.6 15.7 collective-permute-done.11
  1533.6 26.2 %while.77 = (s32[]{:T(128)}, bf16[1413,32,128]{2,1,0:T(8,128)(2,1)}, bf16[1413,32,128]{2,1,0:T(8,128)(2,1)}, s32[]{:T(128)}, s32[]{:T(128)}, /*index=5*/s32[]{:T...) while((s32[]{:T(128)}, bf16[1413,32,128]{2,1,0:T(8,128)(2,1)}, ...), condition=%wide.region_123.124_spmd, body=%wide.region_122.123_spmd.sunk | while | flops 4194320 | bytes 18874736 | solution.py:412
  1559.8 67.7 %take_blocks.1.grad_ref = bf16[1922,32,128]{2,1,0:T(8,128)(2,1)} custom-call(s32[1984]{0:T(1024)} %pad.28.idx_ref, bf16[1412,32,128]{2,1,0:T(8,128)(2,1)} %get-tuple-element.254.refs_0_, bf16[1412,32,128]{2,1,0:T(8,128)(2,1)} %get-tuple-element.255.refs_1_, bf16[1413,32,128]{2,1,0:T(8,128)(2,1)} %get-tuple-element.258.refs_2_, ...), custom_call_target="tpu_custom_call" | custom-call | tf_op jit(solution)/shard_map/take_blocks/pallas_call | solution.py:207
  1627.5 15.6 select_reduce_fusion
  1664.6 80.5 %update.1 = (f32[1922,32,128]{2,1,0:T(8,128)}, f32[1922,32,128]{2,1,0:T(8,128)}, f32[1922,32,128]{2,1,0:T(8,128)}) custom-call(f32[1]{0:T(128)} %bitcast.97.scal_ref, s32[1]{0:T(128)} %bitcast.98.count_ref, bf16[1922,32,128]{2,1,0:T(8,128)(2,1)} %take_blocks.1.grad_ref, f32[1922,32,128]{2,1,0:T(8,128)} %bitcast.264, f32[1922,32,128]{2,1,0:T(8,128)} %bitcast.265, ...), custom_call_target="tpu_custom_call" | custom-call | tf_op jit(solution)/shard_map/update/pallas_call | solution.py:331
  (635 shorter events, 902.9 us)
Async XLA Ops:
  7.2 376.6 %reduce-scatter.5.cloned.1.call-start = ((), (), s32[]{:S(2)}) async-start(), calls=%async_computation.4 | async-start | bytes 4718592 | tf_op jit(solution)/shard_map/reduce_scatter | solution.py:537
  43.6 28.5 %collective-permute-start.17 = (bf16[128,32,128]{2,1,0:T(8,128)(2,1)S(1)}, bf16[128,32,128]{2,1,0:T(8,128)(2,1)}, u32[]{:S(2)}, u32[]{:S(2)}) collective-permute-start(bf16[128,32,128]{2,1,0:T(8,128)(2,1)S(1)} %get-tuple-element.481), channel_id=1, source_target_pairs={{24,8},{16,24},{0,16},{8,0},{25,9},{17,25},{1,17},{9,1},{26,10},{1... | collective-permute-start | bytes 3145736 | tf_op jit(solution)/shard_map/ppermute | solution.py:425
  46.7 32.0 %collective-permute-start.12 = (bf16[128,32,128]{2,1,0:T(8,128)(2,1)S(1)}, bf16[128,32,128]{2,1,0:T(8,128)(2,1)S(1)}, u32[]{:S(2)}, u32[]{:S(2)}) collective-permute-start(bf16[128,32,128]{2,1,0:T(8,128)(2,1)S(1)} %get-tuple-element.482), channel_id=1, source_target_pairs={{8,24},{24,16},{16,0},{0,8},{9,25},{25,17},{17,1},{1,9},{10,26},{2... | collective-permute-start | bytes 3145736 | tf_op jit(solution)/shard_map/ppermute | solution.py:425
  254.2 309.9 %all-gather.12.cloned.1.call-start = ((), (), s32[]{:S(2)}) async-start(), calls=%async_computation.8 | async-start | bytes 4718592 | tf_op jit(solution)/shard_map/all_gather | solution.py:622
  381.7 26.4 %collective-permute-start.31 = (bf16[128,32,128]{2,1,0:T(8,128)(2,1)}, bf16[128,32,128]{2,1,0:T(8,128)(2,1)}, u32[]{:S(2)}, u32[]{:S(2)}) collective-permute-start(bf16[128,32,128]{2,1,0:T(8,128)(2,1)} %get-tuple-element.473), channel_id=1, source_target_pairs={{24,8},{16,24},{0,16},{8,0},{25,9},{17,25},{1,17},{9,1},{26,10},{1... | collective-permute-start | bytes 3145736 | tf_op jit(solution)/shard_map/ppermute | solution.py:425
  382.5 28.7 %collective-permute-start.26 = (bf16[128,32,128]{2,1,0:T(8,128)(2,1)S(1)}, bf16[128,32,128]{2,1,0:T(8,128)(2,1)}, u32[]{:S(2)}, u32[]{:S(2)}) collective-permute-start(bf16[128,32,128]{2,1,0:T(8,128)(2,1)S(1)} %get-tuple-element.474), channel_id=1, source_target_pairs={{8,24},{24,16},{16,0},{0,8},{9,25},{25,17},{17,1},{1,9},{10,26},{2... | collective-permute-start | bytes 3145736 | tf_op jit(solution)/shard_map/ppermute | solution.py:425
  397.6 254.8 %reduce-scatter.7.cloned.1.call-start = ((), (), s32[]{:S(2)}) async-start(), calls=%async_computation.5 | async-start | bytes 4718592 | tf_op jit(solution)/shard_map/reduce_scatter | solution.py:588
  482.3 25.8 %collective-permute-start.35 = (bf16[128,32,128]{2,1,0:T(8,128)(2,1)}, bf16[128,32,128]{2,1,0:T(8,128)(2,1)S(1)}, u32[]{:S(2)}, u32[]{:S(2)}) collective-permute-start(bf16[128,32,128]{2,1,0:T(8,128)(2,1)} %dynamic_slice.391), channel_id=1, source_target_pairs={{24,8},{16,24},{0,16},{8,0},{25,9},{17,25},{1,17},{9,1},{26,10},{1... | collective-permute-start | bytes 3145736 | tf_op jit(solution)/shard_map/ppermute | solution.py:425
  512.5 25.7 %collective-permute-start.5 = (bf16[128,32,128]{2,1,0:T(8,128)(2,1)}, bf16[128,32,128]{2,1,0:T(8,128)(2,1)}, u32[]{:S(2)}, u32[]{:S(2)}) collective-permute-start(bf16[128,32,128]{2,1,0:T(8,128)(2,1)} %constant_dynamic-slice_fusion.39), channel_id=1, source_target_pairs={{24,8},{16,24},{0,16},{8,0},{25,9},{17,25},{1,17},{9,1},{26,10},{1... | collective-permute-start | bytes 3145736 | tf_op jit(solution)/shard_map/while/body/ppermute | solution.py:425
  514.7 25.8 %collective-permute-start.4 = (bf16[128,32,128]{2,1,0:T(8,128)(2,1)S(1)}, bf16[128,32,128]{2,1,0:T(8,128)(2,1)S(1)}, u32[]{:S(2)}, u32[]{:S(2)}) collective-permute-start(bf16[128,32,128]{2,1,0:T(8,128)(2,1)S(1)} %constant_dynamic-slice_fusion.38), channel_id=1, source_target_pairs={{8,24},{24,16},{16,0},{0,8},{9,25},{25,17},{17,1},{1,9},{10,26},{2... | collective-permute-start | bytes 3145736 | tf_op jit(solution)/shard_map/while/body/ppermute | solution.py:425
  602.5 127.8 %reduce-scatter.9.cloned.1.call-start = ((), (), s32[]{:S(2)}) async-start(), calls=%async_computation.6 | async-start | bytes 1179648 | tf_op jit(solution)/shard_map/reduce_scatter | solution.py:661
  699.1 79.4 %all-gather.14.cloned.1.call-start = ((), (), s32[]{:S(2)}) async-start(), calls=%async_computation.9 | async-start | bytes 4718592 | tf_op jit(solution)/shard_map/all_gather | solution.py:668
  733.3 132.0 %reduce-scatter.11.cloned.1.call-start = ((), (), s32[]{:S(2)}) async-start(), calls=%async_computation.7 | async-start | bytes 4718592 | tf_op jit(solution)/shard_map/reduce_scatter | solution.py:588
  816.5 259.8 %all-gather.16.cloned.1.call-start = ((), (), s32[]{:S(2)}) async-start(), calls=%async_computation.10 | async-start | bytes 19021824 | tf_op jit(solution)/shard_map/all_gather | solution.py:733
  900.5 267.3 %all-gather.18.cloned.1.call-start = ((), (), s32[]{:S(2)}) async-start(), calls=%async_computation.11 | async-start | bytes 14155776 | tf_op jit(solution)/shard_map/all_gather | solution.py:732
  961.0 27.0 %collective-permute-start.36 = (bf16[128,32,128]{2,1,0:T(8,128)(2,1)S(1)}, bf16[128,32,128]{2,1,0:T(8,128)(2,1)S(1)}, u32[]{:S(2)}, u32[]{:S(2)}) collective-permute-start(bf16[128,32,128]{2,1,0:T(8,128)(2,1)S(1)} %dynamic_slice.325), channel_id=1, source_target_pairs={{8,24},{24,16},{16,0},{0,8},{9,25},{25,17},{17,1},{1,9},{10,26},{2... | collective-permute-start | bytes 3145736 | tf_op jit(solution)/shard_map/ppermute | solution.py:437
  992.8 47.3 %collective-permute-start.37 = (bf16[128,32,128]{2,1,0:T(8,128)(2,1)}, bf16[128,32,128]{2,1,0:T(8,128)(2,1)}, u32[]{:S(2)}, u32[]{:S(2)}) collective-permute-start(bf16[128,32,128]{2,1,0:T(8,128)(2,1)} %dynamic_slice.392), channel_id=1, source_target_pairs={{8,24},{24,16},{16,0},{0,8},{9,25},{25,17},{17,1},{1,9},{10,26},{2... | collective-permute-start | bytes 3145736 | tf_op jit(solution)/shard_map/ppermute | solution.py:437
  1012.1 32.7 %collective-permute-start.43 = (bf16[128,32,128]{2,1,0:T(8,128)(2,1)}, bf16[128,32,128]{2,1,0:T(8,128)(2,1)}, u32[]{:S(2)}, u32[]{:S(2)}) collective-permute-start(bf16[128,32,128]{2,1,0:T(8,128)(2,1)} %dynamic_slice.397), channel_id=1, source_target_pairs={{24,8},{16,24},{0,16},{8,0},{25,9},{17,25},{1,17},{9,1},{26,10},{1... | collective-permute-start | bytes 3145736 | tf_op jit(solution)/shard_map/ppermute | solution.py:437
  1070.2 259.8 %collective-permute-start.39 = (bf16[128,32,128]{2,1,0:T(8,128)(2,1)}, bf16[128,32,128]{2,1,0:T(8,128)(2,1)S(1)}, u32[]{:S(2)}, u32[]{:S(2)}) collective-permute-start(bf16[128,32,128]{2,1,0:T(8,128)(2,1)} %dynamic_slice.394), channel_id=1, source_target_pairs={{8,24},{24,16},{16,0},{0,8},{9,25},{25,17},{17,1},{1,9},{10,26},{2... | collective-permute-start | bytes 3145736 | tf_op jit(solution)/shard_map/ppermute | solution.py:437
  1074.3 271.6 %collective-permute-start.45 = (bf16[128,32,128]{2,1,0:T(8,128)(2,1)S(1)}, bf16[128,32,128]{2,1,0:T(8,128)(2,1)S(1)}, u32[]{:S(2)}, u32[]{:S(2)}) collective-permute-start(bf16[128,32,128]{2,1,0:T(8,128)(2,1)S(1)} %dynamic_slice.399), channel_id=1, source_target_pairs={{24,8},{16,24},{0,16},{8,0},{25,9},{17,25},{1,17},{9,1},{26,10},{1... | collective-permute-start | bytes 3145736 | tf_op jit(solution)/shard_map/ppermute | solution.py:437
  1243.9 29.1 %collective-permute-start.46 = (bf16[128,32,128]{2,1,0:T(8,128)(2,1)S(1)}, bf16[128,32,128]{2,1,0:T(8,128)(2,1)S(1)}, u32[]{:S(2)}, u32[]{:S(2)}) collective-permute-start(bf16[128,32,128]{2,1,0:T(8,128)(2,1)S(1)} %dynamic_slice.345), channel_id=1, source_target_pairs={{8,24},{24,16},{16,0},{0,8},{9,25},{25,17},{17,1},{1,9},{10,26},{2... | collective-permute-start | bytes 3145736 | tf_op jit(solution)/shard_map/ppermute | solution.py:437
  1300.7 35.0 %collective-permute-start.53 = (bf16[128,32,128]{2,1,0:T(8,128)(2,1)}, bf16[128,32,128]{2,1,0:T(8,128)(2,1)}, u32[]{:S(2)}, u32[]{:S(2)}) collective-permute-start(bf16[128,32,128]{2,1,0:T(8,128)(2,1)} %dynamic_slice.405), channel_id=1, source_target_pairs={{24,8},{16,24},{0,16},{8,0},{25,9},{17,25},{1,17},{9,1},{26,10},{1... | collective-permute-start | bytes 3145736 | tf_op jit(solution)/shard_map/ppermute | solution.py:437
  1306.9 34.4 %collective-permute-start.48 = (bf16[128,32,128]{2,1,0:T(8,128)(2,1)}, bf16[128,32,128]{2,1,0:T(8,128)(2,1)}, u32[]{:S(2)}, u32[]{:S(2)}) collective-permute-start(bf16[128,32,128]{2,1,0:T(8,128)(2,1)} %dynamic_slice.401), channel_id=1, source_target_pairs={{8,24},{24,16},{16,0},{0,8},{9,25},{25,17},{17,1},{1,9},{10,26},{2... | collective-permute-start | bytes 3145736 | tf_op jit(solution)/shard_map/ppermute | solution.py:437
  1328.5 26.1 %collective-permute-start.58 = (bf16[128,32,128]{2,1,0:T(8,128)(2,1)S(1)}, bf16[128,32,128]{2,1,0:T(8,128)(2,1)S(1)}, u32[]{:S(2)}, u32[]{:S(2)}) collective-permute-start(bf16[128,32,128]{2,1,0:T(8,128)(2,1)S(1)} %dynamic_slice.369), channel_id=1, source_target_pairs={{24,8},{16,24},{0,16},{8,0},{25,9},{17,25},{1,17},{9,1},{26,10},{1... | collective-permute-start | bytes 3145736 | tf_op jit(solution)/shard_map/ppermute | solution.py:437
  1335.1 26.1 %collective-permute-start.56 = (bf16[128,32,128]{2,1,0:T(8,128)(2,1)S(1)}, bf16[128,32,128]{2,1,0:T(8,128)(2,1)S(1)}, u32[]{:S(2)}, u32[]{:S(2)}) collective-permute-start(bf16[128,32,128]{2,1,0:T(8,128)(2,1)S(1)} %dynamic_slice.365), channel_id=1, source_target_pairs={{8,24},{24,16},{16,0},{0,8},{9,25},{25,17},{17,1},{1,9},{10,26},{2... | collective-permute-start | bytes 3145736 | tf_op jit(solution)/shard_map/ppermute | solution.py:437
  1339.8 37.3 %collective-permute-start.54 = (bf16[128,32,128]{2,1,0:T(8,128)(2,1)S(1)}, bf16[128,32,128]{2,1,0:T(8,128)(2,1)S(1)}, u32[]{:S(2)}, u32[]{:S(2)}) collective-permute-start(bf16[128,32,128]{2,1,0:T(8,128)(2,1)S(1)} %dynamic_slice.406), channel_id=1, source_target_pairs={{24,8},{16,24},{0,16},{8,0},{25,9},{17,25},{1,17},{9,1},{26,10},{1... | collective-permute-start | bytes 3145736 | tf_op jit(solution)/shard_map/ppermute | solution.py:437
  1345.4 38.2 %collective-permute-start.49 = (bf16[128,32,128]{2,1,0:T(8,128)(2,1)S(1)}, bf16[128,32,128]{2,1,0:T(8,128)(2,1)S(1)}, u32[]{:S(2)}, u32[]{:S(2)}) collective-permute-start(bf16[128,32,128]{2,1,0:T(8,128)(2,1)S(1)} %dynamic_slice.402), channel_id=1, source_target_pairs={{8,24},{24,16},{16,0},{0,8},{9,25},{25,17},{17,1},{1,9},{10,26},{2... | collective-permute-start | bytes 3145736 | tf_op jit(solution)/shard_map/ppermute | solution.py:437
  1348.5 57.6 %collective-permute-start.40 = (bf16[128,32,128]{2,1,0:T(8,128)(2,1)S(1)}, bf16[128,32,128]{2,1,0:T(8,128)(2,1)S(1)}, u32[]{:S(2)}, u32[]{:S(2)}) collective-permute-start(bf16[128,32,128]{2,1,0:T(8,128)(2,1)S(1)} %dynamic_slice.395), channel_id=1, source_target_pairs={{8,24},{24,16},{16,0},{0,8},{9,25},{25,17},{17,1},{1,9},{10,26},{2... | collective-permute-start | bytes 3145736 | tf_op jit(solution)/shard_map/ppermute | solution.py:437
  1358.4 50.3 %collective-permute-start.59 = (bf16[128,32,128]{2,1,0:T(8,128)(2,1)S(1)}, bf16[128,32,128]{2,1,0:T(8,128)(2,1)S(1)}, u32[]{:S(2)}, u32[]{:S(2)}) collective-permute-start(bf16[128,32,128]{2,1,0:T(8,128)(2,1)S(1)} %dynamic_slice.409), channel_id=1, source_target_pairs={{24,8},{16,24},{0,16},{8,0},{25,9},{17,25},{1,17},{9,1},{26,10},{1... | collective-permute-start | bytes 3145736 | tf_op jit(solution)/shard_map/ppermute | solution.py:437
  1364.9 63.6 %collective-permute-start.57 = (bf16[128,32,128]{2,1,0:T(8,128)(2,1)S(1)}, bf16[128,32,128]{2,1,0:T(8,128)(2,1)S(1)}, u32[]{:S(2)}, u32[]{:S(2)}) collective-permute-start(bf16[128,32,128]{2,1,0:T(8,128)(2,1)S(1)} %dynamic_slice.408), channel_id=1, source_target_pairs={{8,24},{24,16},{16,0},{0,8},{9,25},{25,17},{17,1},{1,9},{10,26},{2... | collective-permute-start | bytes 3145736 | tf_op jit(solution)/shard_map/ppermute | solution.py:437
  1380.8 50.2 %collective-permute-start.55 = (bf16[128,32,128]{2,1,0:T(8,128)(2,1)S(1)}, bf16[128,32,128]{2,1,0:T(8,128)(2,1)S(1)}, u32[]{:S(2)}, u32[]{:S(2)}) collective-permute-start(bf16[128,32,128]{2,1,0:T(8,128)(2,1)S(1)} %dynamic_slice.407), channel_id=1, source_target_pairs={{24,8},{16,24},{0,16},{8,0},{25,9},{17,25},{1,17},{9,1},{26,10},{1... | collective-permute-start | bytes 3145736 | tf_op jit(solution)/shard_map/ppermute | solution.py:437
  1387.4 60.4 %collective-permute-start.50 = (bf16[128,32,128]{2,1,0:T(8,128)(2,1)S(1)}, bf16[128,32,128]{2,1,0:T(8,128)(2,1)S(1)}, u32[]{:S(2)}, u32[]{:S(2)}) collective-permute-start(bf16[128,32,128]{2,1,0:T(8,128)(2,1)S(1)} %dynamic_slice.403), channel_id=1, source_target_pairs={{8,24},{24,16},{16,0},{0,8},{9,25},{25,17},{17,1},{1,9},{10,26},{2... | collective-permute-start | bytes 3145736 | tf_op jit(solution)/shard_map/ppermute | solution.py:437
  (131 other events, 2887.7 us)
Sparse Core Ops, SparseCore 0:
  254.3 49.4 reduce-scatter.4
  397.7 46.3 all-gather.11
  602.6 49.7 reduce-scatter.6
  699.2 31.0 reduce-scatter.8
  733.4 44.9 all-gather.13
  816.6 48.7 reduce-scatter.10
  900.6 150.6 all-gather.15
  1052.9 114.8 all-gather.17

commit v3 on v2

--- a/solution.py
+++ b/solution.py
@@ -31,7 +31,7 @@
 ROPE_BASE = 10000.0
 MASK_FILL = -1e30
 LANES = 128
-CHUNK = 128
+FRESH = 256
 BATCH = 64
 
 
@@ -198,15 +198,15 @@
         fetch(i + 1, 1 - slot)
 
     pltpu.make_async_copy(sources[0].at[pl.ds(0, BATCH)], buf.at[slot], sem.at[slot]).wait()
-    out_ref[...] = buf[slot]
-
-
-def take_blocks(streams, index):
+    out_ref[...] = buf[slot].astype(jnp.float32)
+
+
+def take_blocks(streams, index, extra=0):
     count = index.shape[0]
     sub = streams[0].shape[1]
     return pl.pallas_call(
         functools.partial(own_kernel, tuple(s.shape[0] for s in streams)),
-        out_shape=jax.ShapeDtypeStruct((count, sub, LANES), jnp.bfloat16),
+        out_shape=jax.ShapeDtypeStruct((count + extra, sub, LANES), jnp.float32),
         grid_spec=pltpu.PrefetchScalarGridSpec(
             num_scalar_prefetch=1,
             grid=(pl.cdiv(count, BATCH),),
@@ -342,10 +342,10 @@
 
 
 class Part:
-    def __init__(self, lo, hi, member, before, counts_before, ring_pos, my_pos):
+    def __init__(self, lo, hi, chunk, member, before, counts_before, ring_pos, my_pos):
         groups = member.shape[1]
-        self.lo, self.count, self.groups = lo, hi - lo, groups
-        self.size = (hi - lo) // 2 + groups + (groups + 1) * CHUNK
+        self.lo, self.count, self.groups, self.chunk = lo, hi - lo, groups, chunk
+        self.size = (hi - lo) // 2 + groups + (groups + 1) * chunk
         inside = member[lo:hi]
         self.held = jnp.sum(inside, axis=0)
         self.base = counts_before
@@ -359,7 +359,7 @@
         steps = jnp.zeros((), jnp.int32)
         slots = jnp.arange(groups, dtype=jnp.int32)
         for way in (0, 1):
-            wide = jnp.maximum(halves[way], CHUNK)
+            wide = jnp.maximum(halves[way], chunk)
             at_ring = jnp.sum(jnp.where(ring_pos[None, :] == slots[:, None], wide[None, :], 0), axis=1)
             steps = jnp.maximum(steps, jnp.max(jnp.sum(at_ring) - at_ring))
             turn = 1 if way == 0 else -1
@@ -380,8 +380,8 @@
             self.scatter_lag.append(prev)
             self.gather_seg.append(by_group(starts(my_pos)))
             self.scatter_seg.append(by_group(starts((my_pos - turn) % groups)))
-        self.dyn_steps = (steps + CHUNK - 1) // CHUNK
-        self.fixed_steps = int(0.45 * (hi - lo)) // CHUNK
+        self.dyn_steps = (steps + chunk - 1) // chunk
+        self.fixed_steps = pl.cdiv(int(0.46 * (hi - lo)), chunk)
 
         def place(seg):
             up = jnp.sum((seg[0])[None, :] * inside, axis=1) + rank
@@ -421,9 +421,9 @@
     ]
 
     def step(s, way, stream):
-        sent = lax.dynamic_slice_in_dim(stream, s * CHUNK, CHUNK)
+        sent = lax.dynamic_slice_in_dim(stream, s * part.chunk, part.chunk)
         got = lax.ppermute(sent, "grp", links[way])
-        at = jnp.minimum(part.lag[way] + s * CHUNK, part.size - CHUNK)
+        at = jnp.minimum(part.lag[way] + s * part.chunk, part.size - part.chunk)
         return lax.dynamic_update_slice_in_dim(stream, got, at, 0)
 
     return run_ring(part, streams, step)
@@ -433,10 +433,10 @@
     links = ring_links(part.groups)
 
     def step(s, way, stream):
-        sent = lax.dynamic_slice_in_dim(stream, s * CHUNK, CHUNK)
+        sent = lax.dynamic_slice_in_dim(stream, s * part.chunk, part.chunk)
         got = lax.ppermute(sent, "grp", links[way])
-        at = jnp.minimum(part.scatter_lag[way] + s * CHUNK, part.size - CHUNK)
-        old = lax.dynamic_slice_in_dim(stream, at, CHUNK)
+        at = jnp.minimum(part.scatter_lag[way] + s * part.chunk, part.size - part.chunk)
+        old = lax.dynamic_slice_in_dim(stream, at, part.chunk)
         total = (old.astype(jnp.float32) + got.astype(jnp.float32)).astype(jnp.bfloat16)
         return lax.dynamic_update_slice_in_dim(stream, total, at, 0)
 
@@ -504,20 +504,21 @@
     member = (owners[:, None] == jnp.arange(groups, dtype=jnp.int32)[None, :]).astype(jnp.int32)
     before = jnp.cumsum(member, axis=0) - member
     marks = [0, (gu_size + dn_size) // row_width, col_size // row_width, blocks]
+    chunks = [144, 144, 104]
     parts = []
     counts_before = jnp.zeros((groups,), jnp.int32)
-    for lo, hi in zip(marks[:-1], marks[1:]):
-        parts.append(Part(lo, hi, member, before, counts_before, ring_pos, my_pos))
+    for lo, hi, chunk in zip(marks[:-1], marks[1:], chunks):
+        parts.append(Part(lo, hi, chunk, member, before, counts_before, ring_pos, my_pos))
         counts_before = counts_before + parts[-1].held
     exp_part, tab_part, att_part = parts
     master_rows = master_weights.reshape(capacity, sub, LANES)
     own = cast_rows(master_rows, max(part.size for part in parts))
-    tab_streams = ring_gather(tab_part, own, group_index)
-    own, tab_streams = lax.optimization_barrier((own, tab_streams))
+    att_streams = ring_gather(att_part, own, group_index)
+    own_next, att_streams = lax.optimization_barrier((own, att_streams))
+    exp_streams = ring_gather(exp_part, own_next, group_index)
+    own_next, exp_streams = lax.optimization_barrier((own_next, exp_streams))
+    tab_streams = ring_gather(tab_part, own_next, group_index)
     table = unpack(tab_streams, tab_part.gather_place)
-    att_streams = ring_gather(att_part, own, group_index)
-    own, att_streams = lax.optimization_barrier((own, att_streams))
-    exp_streams = ring_gather(exp_part, own, group_index)
     gu_nb = gu_size // row_width
     gate_up = unpack(exp_streams, exp_part.gather_place[:gu_nb]).reshape(local_experts, D, 2 * FF)
     down = unpack(exp_streams, exp_part.gather_place[gu_nb:]).reshape(local_experts, FF, D)
@@ -532,8 +533,73 @@
     group_ids = token_ids.reshape(shards * length)
     local_ids = group_ids - shard_index * vocab_rows
     inside = (local_ids >= 0) & (local_ids < vocab_rows)
-    safe_ids = jnp.clip(local_ids, 0, vocab_rows - 1)
-    found = jnp.where(inside[:, None], table[safe_ids], jnp.zeros((), jnp.bfloat16))
+    order_ids = jnp.arange(shards * length, dtype=jnp.int32)
+    same = group_ids[:, None] == group_ids[None, :]
+    first = ~jnp.any(same & (order_ids[None, :] < order_ids[:, None]), axis=1)
+    shard_of = group_ids // vocab_rows
+    most = jnp.max(
+        jnp.sum(
+            (first[:, None] & (shard_of[:, None] == jnp.arange(shards)[None, :])).astype(jnp.int32),
+            axis=0,
+        )
+    )
+    own_first = (first & inside).astype(jnp.int32)
+    first_slot = jnp.cumsum(own_first) - own_first
+    token_slot = jnp.sum(jnp.where(same & (own_first[None, :] > 0), first_slot[None, :], 0), axis=1)
+    token_slot = jnp.where(inside, token_slot, -1)
+    most = jnp.max(lax.all_gather(most.reshape(1), "grp", axis=0))
+    rounds = (most + FRESH - 1) // FRESH
+    tab_rank = jnp.sum(
+        jnp.where(
+            jnp.arange(groups, dtype=jnp.int32)[None, :] == group_index,
+            jnp.where(member > 0, before, -1),
+            0,
+        ),
+        axis=1,
+    )[marks[1] : marks[2]]
+    rows_a_block = row_width // D
+    row_tile = D // LANES
+    own_rows = own.reshape(own.shape[0] * rows_a_block, row_tile, LANES)
+    slot_range = jnp.arange(FRESH, dtype=jnp.int32)
+
+    def wanted(turn):
+        mine = (own_first[None, :] > 0) & (
+            first_slot[None, :] == (turn * FRESH + slot_range)[:, None]
+        )
+        listed = jnp.sum(jnp.where(mine, local_ids[None, :] + 1, 0), axis=1) - 1
+        listed = lax.all_gather(listed, "grp", axis=0)
+        rank = tab_rank[jnp.maximum(listed, 0) // rows_a_block]
+        here = (listed >= 0) & (rank >= 0)
+        return jnp.where(here, rank * rows_a_block + listed % rows_a_block, -1)
+
+    def spread(turn):
+        return (
+            token_slot[:, None] == (turn * FRESH + slot_range)[None, :]
+        ).astype(jnp.bfloat16)
+
+    def shifted(shift):
+        return [(g, (g + shift) % groups) for g in range(groups)]
+
+    def fresh_rows(turn, want):
+        flat = want.reshape(-1)
+        supply = jnp.where(
+            (flat >= 0)[:, None, None], own_rows[jnp.maximum(flat, 0)], jnp.zeros((), jnp.bfloat16)
+        ).reshape(groups, FRESH, row_tile, LANES)
+        rows_now = lax.dynamic_index_in_dim(supply, group_index, 0, keepdims=False)
+        for shift in range(1, groups):
+            away = lax.dynamic_index_in_dim(
+                supply, (group_index + shift) % groups, 0, keepdims=False
+            )
+            rows_now = rows_now + lax.ppermute(away, "grp", shifted(shift))
+        return jnp.dot(
+            spread(turn), rows_now.reshape(FRESH, D), preferred_element_type=jnp.float32
+        ).astype(jnp.bfloat16)
+
+    want_now = wanted(0)
+    found = fresh_rows(0, want_now)
+    found = lax.fori_loop(
+        1, rounds, lambda turn, so_far: so_far + fresh_rows(turn, wanted(turn)), found
+    )
     x_embed = embed_scale * lax.psum_scatter(found, "ep", scatter_dimension=0, tiled=True).astype(
         jnp.float32
     )
@@ -657,6 +723,7 @@
         jnp.bfloat16
     )
     grad_table = jnp.einsum("av,ad->vd", d_logits, group_rows, preferred_element_type=jnp.float32)
+    tab_sums = ring_scatter(tab_part, pack(grad_table, tab_part.scatter_place, tab_part.size))
     head_part = jnp.einsum("av,vd->ad", d_logits, table, preferred_element_type=jnp.float32)
     grad_picked = lax.psum_scatter(head_part, "ep", scatter_dimension=0, tiled=True)
     grad_value = 2.0 * VALUE_COEF * (value_pred - own_targets) / npos
@@ -750,30 +817,54 @@
         axis=(0, 1),
     )
     att_grads = (grad_w_query, grad_w_keyval, grad_w_out, grad_gains)
-    grad_table = grad_table + jax.ops.segment_sum(
-        jnp.where(inside[:, None], all_rows.astype(jnp.float32), 0.0),
-        safe_ids,
-        num_segments=vocab_rows,
-    )
     att_rows = jnp.concatenate([piece.reshape(-1, D) for piece in att_grads], axis=0)
     exp_sums = pack(grad_gate_up.reshape(-1, D), exp_part.scatter_place[:gu_nb], exp_part.size)
     exp_sums = pack(
         grad_down.reshape(-1, D), exp_part.scatter_place[gu_nb:], exp_part.size, exp_sums
     )
+    tab_sums, exp_sums = lax.optimization_barrier((tab_sums, exp_sums))
     exp_sums = ring_scatter(exp_part, exp_sums)
-    tab_sums = ring_scatter(tab_part, pack(grad_table, tab_part.scatter_place, tab_part.size))
-    att_sums = ring_scatter(att_part, pack(att_rows, att_part.scatter_place, att_part.size))
     row = jnp.arange(capacity, dtype=jnp.int32)
     valid = pick(counts_before, group_index)
+    own_col = pick(att_part.base, group_index)
+    in_exp, place = own_index(exp_part, group_index, row, 0)
+    in_tab, tab_place = own_index(tab_part, group_index, row, 2 * exp_part.size)
+    place = jnp.where(in_exp, place, jnp.where(in_tab, tab_place, 0))
+    owned = take_blocks((*exp_sums, *tab_sums), place, att_part.count)
+
+    def add_fresh(turn, want, so_far):
+        sums = jnp.einsum(
+            "nk,nd->kd", spread(turn), all_rows, preferred_element_type=jnp.float32
+        ).astype(jnp.bfloat16)
+        sums = sums.reshape(FRESH, row_tile, LANES)
+        gone = so_far.shape[0]
+        for shift in range(groups):
+            came = lax.ppermute(sums, "grp", shifted(shift)) if shift else sums
+            at = lax.dynamic_index_in_dim(
+                want, (group_index - shift) % groups, 0, keepdims=False
+            )
+            so_far = so_far.at[jnp.where(at >= 0, at, gone)].add(
+                came.astype(jnp.float32), mode="drop"
+            )
+        return so_far
+
+    owned_rows = owned.reshape(owned.shape[0] * rows_a_block, row_tile, LANES)
+    owned_rows = add_fresh(0, want_now, owned_rows)
+    owned_rows = lax.fori_loop(
+        1, rounds, lambda turn, so_far: add_fresh(turn, wanted(turn), so_far), owned_rows
+    )
+    owned = owned_rows.reshape(owned.shape)
+    exp_sums, att_grad_streams = lax.optimization_barrier(
+        (exp_sums, pack(att_rows, att_part.scatter_place, att_part.size))
+    )
+    att_sums = ring_scatter(att_part, att_grad_streams)
+    _, att_place = own_index(
+        att_part, group_index, own_col + jnp.arange(att_part.count, dtype=jnp.int32), 0
+    )
+    att_place = jnp.clip(att_place, 0, 2 * att_part.size - 1)
+    owned = lax.dynamic_update_slice_in_dim(owned, take_blocks(att_sums, att_place), own_col, 0)
     filled = row < valid
-    own_col = pick(att_part.base, group_index)
-    place = jnp.zeros((capacity,), jnp.int32)
-    offset = 0
-    for part in (exp_part, tab_part, att_part):
-        inside_part, at = own_index(part, group_index, row, offset)
-        place = jnp.where(inside_part, at, place)
-        offset += 2 * part.size
-    owned = take_blocks((*exp_sums, *tab_sums, *att_sums), place)
+    owned = owned[:capacity]
     counted = (filled & ((row < own_col) | (shard_index == 0))).reshape(capacity, 1, 1)
     wide_owned = owned.astype(jnp.float32)
     square = jnp.sum(jnp.where(counted, wide_owned * wide_owned, 0.0))

time: 1780 us -> 1770 us (level)
  waiting for transfers between devices: 651 us -> 447 us
  other arithmetic: 212 us -> 316 us
  starting transfers between devices: 71.1 us -> 137 us
  blocking collectives: 43.2 us -> 77 us
    all_gather x1, waiting for transfers between devices: 85.9 us -> 0.02 us  [on_device(): lax.all_gather(jnp.concatenate([attended, normed_q, normed], axis=0), 'ep...]
    scatter-add x1 -> x4, other arithmetic: 35.9 us -> 107 us  [add_fresh(): so_far.at[jnp.where(at >= 0, at, gone)]]
    ppermute x64 -> x56, waiting for transfers between devices: 376 us -> 312 us  [step(): got = lax.ppermute(sent, 'grp', links[way])]
    ppermute x5, starting transfers between devices: 0.7 us -> 63.2 us  [sum_everywhere(): values = values + lax.ppermute(values, axis, pairs)]
    reduce_scatter x2, waiting for transfers between devices: 97.9 us -> 48 us  [from_experts(): lax.psum_scatter(partial.reshape(shards * rows, D), 'ep', scatter_dimensi...]
    slice x0 -> x1, other arithmetic: none -> 27.8 us  [on_device(): owned = owned[:capacity]]
    pallas_call x1 -> x2, Pallas kernels: 67.7 us -> 53.5 us  [take_blocks(): pl.pallas_call(functools.partial(own_kernel, tuple((s.shape[0] for s in s...]
    dynamic_slice x61 -> x53, local copies, waits for them, and re-layouts: 101 us -> 88.8 us  [step(): sent = lax.dynamic_slice_in_dim(stream, s * part.chunk, part.chunk)]
  transfers between devices with their start and end apart: 77 -> 75, of which waited for: 46 -> 43; matrix products, arithmetic and copies ran while one was open for 22% -> 30% of each run, Pallas kernels for 6% -> 9%
where the time goes in v3:
time: 1770 us; the launch traced here: 1750 us
  waiting for transfers between devices  447 us (25%)
  other arithmetic  316 us (18%)
  Pallas kernels  298 us (17%)
  local copies, waits for them, and re-layouts  231 us (13%)
  matrix products  168 us (9%)
  starting transfers between devices  137 us (8%)
  blocking collectives  77 us (4%)
  between operations  70.2 us (4%)
    ppermute x56, waiting for transfers between devices, step(): got = lax.ppermute(sent, 'grp', links[way])  312 us
    scatter-add x4, other arithmetic, add_fresh(): so_far.at[jnp.where(at >= 0, at, gone)]  107 us
    dynamic_slice x53, local copies, waits for them, and re-layouts, step(): sent = lax.dynamic_slice_in_dim(stream, s * part.chunk, part.chunk)  88.8 us
    pallas_call x1, Pallas kernels, update(): pl.pallas_call(update_kernel, out_shape=(shape, shape, shape), grid_spec=...  82.4 us
    dynamic_update_slice x28, other arithmetic, step(): return lax.dynamic_update_slice_in_dim(stream, total, at, 0)  75.4 us
    pallas_call x4, Pallas kernels, pack(): pl.pallas_call(functools.partial(pack_kernel, count, keep), out_shape=(sh...  68.5 us
    pallas_call x7, Pallas kernels, unpack(): pl.pallas_call(unpack_kernel, out_shape=jax.ShapeDtypeStruct((count * row...  65.6 us
    ppermute x56, starting transfers between devices, step(): got = lax.ppermute(sent, 'grp', links[way])  64.5 us
  transfers between devices with their start and end apart: 75, of which 43 were waited for; matrix products, arithmetic and copies ran while one was open for 30% of the time, Pallas kernels for 9%

profile of v3, /device:TPU:0, one launch (start us, length us, event | category | flops | bytes accessed | tf_op | source)
XLA Modules:
  0.0 1745.8 jit_solution(7181088134896230531)
XLA Ops:
  14.3 27.5 %cast_rows.1 = bf16[3415,32,128]{2,1,0:T(8,128)(2,1)} custom-call(f32[1922,32,128]{2,1,0:T(8,128)} %bitcast.457), custom_call_target="tpu_custom_call" | custom-call | tf_op jit(solution)/shard_map/cast_rows/pallas_call | solution.py:87
  54.6 16.3 all-gather.11
  104.1 17.2 all-reduce.8
  350.2 14.4 all-gather.3
  382.9 14.4 unpack.12
  461.0 16.1 collective-permute-done.45
  492.3 15.6 collective-permute-done.46
  577.7 23.2 %unpack.13 = bf16[6152,1024]{1,0:T(8,128)(2,1)} custom-call(s32[1600]{0:T(1024)} %pad.35.idx_ref, bf16[1493,32,128]{2,1,0:T(8,128)(2,1)} %get-tuple-element.860.first_ref, bf16[1493,32,128]{2,1,0:T(8,128)(2,1)} %get-tuple-element.861.second_ref), custom_call_target="tpu_custom_call" | custom-call | bytes 25198592 | tf_op jit(solution)/shard_map/unpack/pallas_call | solution.py:148
  604.2 15.1 all_gather.68
  648.5 32.3 %reduce-scatter.9.cloned.1.call-done = f32[32,1024]{1,0:T(8,128)} async-done(((f32[256,1024]{1,0:T(8,128)}), f32[32,1024]{1,0:T(8,128)}) %reduce-scatter.9.cloned.1.call-update) | async-done | bytes 131088 | tf_op jit(solution)/shard_map/reduce_scatter | solution.py:728
  684.3 44.8 %all-gather.26.cloned.1.call-done = bf16[2048,1024]{1,0:T(8,128)(2,1)} async-done(((bf16[256,1024]{1,0:T(8,128)(2,1)}), bf16[2048,1024]{1,0:T(8,128)(2,1)}) %all-gather.26.cloned.1.call-update) | async-done | bytes 4194320 | tf_op jit(solution)/shard_map/all_gather | solution.py:735
  768.0 48.0 %reduce-scatter.11.cloned.1.call-done = bf16[256,1024]{1,0:T(8,128)(2,1)} async-done(((bf16[2048,1024]{1,0:T(8,128)(2,1)}), bf16[256,1024]{1,0:T(8,128)(2,1)}) %reduce-scatter.11.cloned.1.call-update) | async-done | bytes 524304 | tf_op jit(solution)/shard_map/reduce_scatter | solution.py:654
  849.9 15.0 fusion.254.src_ref
  864.9 26.1 %pack.4 = (bf16[1493,32,128]{2,1,0:T(8,128)(2,1)}, bf16[1493,32,128]{2,1,0:T(8,128)(2,1)}) custom-call(s32[1600]{0:T(1024)} %pad.33.idx_ref, f32[6152,1024]{1,0:T(8,128)} %fusion.254.src_ref), custom_call_target="tpu_custom_call" | custom-call | bytes 37797888 | tf_op jit(solution)/shard_map/pack/pallas_call | solution.py:283
  900.1 20.1 %collective-permute-done.54 = bf16[144,32,128]{2,1,0:T(8,128)(2,1)} collective-permute-done((bf16[144,32,128]{2,1,0:T(8,128)(2,1)}, bf16[144,32,128]{2,1,0:T(8,128)(2,1)}, u32[]{:S(2)}, u32[]{:S(2)}) %collective-permute-start.54) | collective-permute-done | bytes 1179680 | tf_op jit(solution)/shard_map/ppermute | solution.py:437
  932.8 17.6 %collective-permute-done.55 = bf16[144,32,128]{2,1,0:T(8,128)(2,1)} collective-permute-done((bf16[144,32,128]{2,1,0:T(8,128)(2,1)S(1)}, bf16[144,32,128]{2,1,0:T(8,128)(2,1)}, u32[]{:S(2)}, u32[]{:S(2)}) %collective-permute-start.55) | collective-permute-done | bytes 1179680 | tf_op jit(solution)/shard_map/ppermute | solution.py:437
  962.5 17.0 collective-permute-done.56
  991.5 16.1 collective-permute-done.57
  1056.9 18.2 %pack.5 = (bf16[1492,32,128]{2,1,0:T(8,128)(2,1)}, bf16[1492,32,128]{2,1,0:T(8,128)(2,1)}) custom-call(s32[1024]{0:T(1024)} %slice.280.idx_ref, f32[4096,1024]{1,0:T(8,128)} %bitcast.465), custom_call_target="tpu_custom_call" | custom-call | bytes 25165824 | tf_op jit(solution)/shard_map/pack/pallas_call | solution.py:283
  1100.6 17.1 collective-permute-done.64
  1181.6 14.2 collective-permute-done.67
  1283.8 14.5 collective-permute-done.76
  1367.6 38.3 %take_blocks.2 = f32[2691,32,128]{2,1,0:T(8,128)} custom-call(s32[1984]{0:T(1024)} %pad.31.idx_ref, bf16[1492,32,128]{2,1,0:T(8,128)(2,1)} %get-tuple-element.872.refs_0_, bf16[1492,32,128]{2,1,0:T(8,128)(2,1)} %get-tuple-element.873.refs_1_, bf16[1493,32,128]{2,1,0:T(8,128)(2,1)} %get-tuple-element.874.refs_2_, ...), custom_call_target="tpu_custom_call" | custom-call | tf_op jit(solution)/shard_map/take_blocks/pallas_call | solution.py:207
  1405.9 27.3 %scatter_fusion.4 = f32[10764,8,128]{2,1,0:T(8,128)} fusion(f32[10764,8,128]{2,1,0:T(8,128)} %bitcast.454, s32[256]{0:T(256)S(1)} %bitcast.552, f32[256,8,128]{2,1,0:T(8,128)S(1)} %bitcast_convert_fusion.3), kind=kCustom, calls=%fused_computation.11 | custom fusion | flops 262144 | bytes 3146752 | tf_op jit(solution)/shard_map/scatter-add | solution.py:846
  1434.3 26.6 %scatter_fusion.5 = f32[10764,8,128]{2,1,0:T(8,128)} fusion(f32[10764,8,128]{2,1,0:T(8,128)} %scatter_fusion.4, s32[256]{0:T(256)S(1)} %bitcast.551, f32[256,8,128]{2,1,0:T(8,128)S(1)} %convert_element_type.715), kind=kCustom, calls=%fused_computation.12 | custom fusion | flops 262144 | bytes 3146752 | tf_op jit(solution)/shard_map/scatter-add | solution.py:846
  1462.0 26.7 %scatter_fusion.6 = f32[10764,8,128]{2,1,0:T(8,128)} fusion(f32[10764,8,128]{2,1,0:T(8,128)} %scatter_fusion.5, s32[256]{0:T(256)S(1)} %bitcast.550, f32[256,8,128]{2,1,0:T(8,128)S(1)} %convert_element_type.716), kind=kCustom, calls=%fused_computation.13 | custom fusion | flops 262144 | bytes 3146752 | tf_op jit(solution)/shard_map/scatter-add | solution.py:846
  1489.9 26.6 %scatter_fusion.7 = f32[10764,8,128]{2,1,0:T(8,128)} fusion(f32[10764,8,128]{2,1,0:T(8,128)} %scatter_fusion.6, s32[256]{0:T(256)S(1)} %bitcast.549, f32[256,8,128]{2,1,0:T(8,128)S(1)} %convert_element_type.717), kind=kCustom, calls=%fused_computation.14 | custom fusion | flops 262144 | bytes 3146752 | tf_op jit(solution)/shard_map/scatter-add | solution.py:846
  1521.3 15.2 take_blocks.3
  1547.6 27.8 %fusion.260 = (f32[1922,32,128]{2,1,0:T(8,128)}, f32[]{:T(128)}) fusion(f32[2691,32,128]{2,1,0:T(8,128)} %constant_dynamic-update-slice_fusion.6, pred[1922]{0:T(1024)(128)(4,1)S(1)} %fusion.212), kind=kLoop, calls=%fused_computation.679 | loop fusion | flops 23617536 | bytes 62982024 | tf_op jit(solution)/shard_map/slice | solution.py:867
  1579.4 24.9 %collective-permute-start.81 = (f32[8,128]{1,0:T(8,128)S(1)}, f32[8,128]{1,0:T(8,128)S(1)}, u32[]{:S(2)}, u32[]{:S(2)}) collective-permute-start(f32[8,128]{1,0:T(8,128)S(1)} %add.1779), channel_id=1, source_target_pairs={{0,2},{1,3},{2,0},{3,1},{4,6},{5,7},{6,4},{7,5},{8,10},{9,11},{10,... | collective-permute-start | bytes 12296 | tf_op jit(solution)/shard_map/ppermute | solution.py:462
  1610.4 25.7 %collective-permute-start.83 = (f32[8,128]{1,0:T(8,128)S(1)}, f32[8,128]{1,0:T(8,128)S(1)}, u32[]{:S(2)}, u32[]{:S(2)}) collective-permute-start(f32[8,128]{1,0:T(8,128)S(1)} %add.1781), channel_id=1, source_target_pairs={{0,8},{8,0},{16,24},{24,16},{1,9},{9,1},{17,25},{25,17},{2,10},{10... | collective-permute-start | bytes 12296 | tf_op jit(solution)/shard_map/ppermute | solution.py:462
  1653.9 82.4 %update.1 = (f32[1922,32,128]{2,1,0:T(8,128)}, f32[1922,32,128]{2,1,0:T(8,128)}, f32[1922,32,128]{2,1,0:T(8,128)}) custom-call(f32[1]{0:T(128)} %bitcast.117.scal_ref, s32[1]{0:T(128)} %bitcast.118.count_ref, f32[1922,32,128]{2,1,0:T(8,128)} %get-tuple-element.1215.grad_ref, f32[1922,32,128]{2,1,0:T(8,128)} %bitcast.458, f32[1922,32,128]{2,1,0:T(8,128)} %bitcast.463, ...), custom_call_target="tpu_custom_call" | custom-call | tf_op jit(solution)/shard_map/update/pallas_call | solution.py:331
  (726 shorter events, 893.5 us)
Async XLA Ops:
  7.2 265.1 %reduce-scatter.5.cloned.1.call-start = ((), (), s32[]{:S(2)}) async-start(), calls=%async_computation.4 | async-start | bytes 4718592 | tf_op jit(solution)/shard_map/reduce_scatter | solution.py:603
  45.3 100.4 %collective-permute-start.25 = (bf16[104,32,128]{2,1,0:T(8,128)(2,1)}, bf16[104,32,128]{2,1,0:T(8,128)(2,1)}, u32[]{:S(2)}, u32[]{:S(2)}) collective-permute-start(bf16[104,32,128]{2,1,0:T(8,128)(2,1)} %get-tuple-element.1225), channel_id=1, source_target_pairs={{24,8},{16,24},{0,16},{8,0},{25,9},{17,25},{1,17},{9,1},{26,10},{1... | collective-permute-start | bytes 2555912 | tf_op jit(solution)/shard_map/ppermute | solution.py:425
  94.9 39.7 %collective-permute-start.18 = (bf16[256,8,128]{2,1,0:T(8,128)(2,1)S(1)}, bf16[256,8,128]{2,1,0:T(8,128)(2,1)S(1)}, u32[]{:S(2)}, u32[]{:S(2)}) collective-permute-start(bf16[256,8,128]{2,1,0:T(8,128)(2,1)S(1)} %get-tuple-element.1231), channel_id=1, source_target_pairs={{0,8},{8,16},{16,24},{24,0},{1,9},{9,17},{17,25},{25,1},{2,10},{10... | collective-permute-start | bytes 1572872 | tf_op jit(solution)/shard_map/ppermute | solution.py:593
  95.2 39.4 %collective-permute-start.20 = (bf16[256,8,128]{2,1,0:T(8,128)(2,1)S(1)}, bf16[256,8,128]{2,1,0:T(8,128)(2,1)S(1)}, u32[]{:S(2)}, u32[]{:S(2)}) collective-permute-start(bf16[256,8,128]{2,1,0:T(8,128)(2,1)S(1)} %get-tuple-element.1232), channel_id=1, source_target_pairs={{0,24},{8,0},{16,8},{24,16},{1,25},{9,1},{17,9},{25,17},{2,26},{10... | collective-permute-start | bytes 1572872 | tf_op jit(solution)/shard_map/ppermute | solution.py:593
  97.9 36.7 %collective-permute-start.19 = (bf16[256,8,128]{2,1,0:T(8,128)(2,1)S(1)}, bf16[256,8,128]{2,1,0:T(8,128)(2,1)S(1)}, u32[]{:S(2)}, u32[]{:S(2)}) collective-permute-start(bf16[256,8,128]{2,1,0:T(8,128)(2,1)S(1)} %get-tuple-element.1233), channel_id=1, source_target_pairs={{0,16},{8,24},{16,0},{24,8},{1,17},{9,25},{17,1},{25,9},{2,18},{10... | collective-permute-start | bytes 1572872 | tf_op jit(solution)/shard_map/ppermute | solution.py:593
  138.7 258.7 %all-gather.24.cloned.1.call-start = ((), (), s32[]{:S(2)}) async-start(), calls=%async_computation.8 | async-start | bytes 4718592 | tf_op jit(solution)/shard_map/all_gather | solution.py:688
  237.4 25.9 %collective-permute-start.29 = (bf16[144,32,128]{2,1,0:T(8,128)(2,1)S(1)}, bf16[144,32,128]{2,1,0:T(8,128)(2,1)S(1)}, u32[]{:S(2)}, u32[]{:S(2)}) collective-permute-start(bf16[144,32,128]{2,1,0:T(8,128)(2,1)S(1)} %get-tuple-element.1222), channel_id=1, source_target_pairs={{8,24},{24,16},{16,0},{0,8},{9,25},{25,17},{17,1},{1,9},{10,26},{2... | collective-permute-start | bytes 3538952 | tf_op jit(solution)/shard_map/ppermute | solution.py:425
  261.8 25.6 %collective-permute-start.35 = (bf16[144,32,128]{2,1,0:T(8,128)(2,1)}, bf16[144,32,128]{2,1,0:T(8,128)(2,1)S(1)}, u32[]{:S(2)}, u32[]{:S(2)}) collective-permute-start(bf16[144,32,128]{2,1,0:T(8,128)(2,1)} %dynamic_slice.532), channel_id=1, source_target_pairs={{24,8},{16,24},{0,16},{8,0},{25,9},{17,25},{1,17},{9,1},{26,10},{1... | collective-permute-start | bytes 3538952 | tf_op jit(solution)/shard_map/ppermute | solution.py:425
  286.2 314.8 %reduce-scatter.7.cloned.1.call-start = ((), (), s32[]{:S(2)}) async-start(), calls=%async_computation.5 | async-start | bytes 4718592 | tf_op jit(solution)/shard_map/reduce_scatter | solution.py:654
  372.7 73.6 %collective-permute-start.44 = (bf16[144,32,128]{2,1,0:T(8,128)(2,1)S(1)}, bf16[144,32,128]{2,1,0:T(8,128)(2,1)}, u32[]{:S(2)}, u32[]{:S(2)}) collective-permute-start(bf16[144,32,128]{2,1,0:T(8,128)(2,1)S(1)} %get-tuple-element.1217), channel_id=1, source_target_pairs={{24,8},{16,24},{0,16},{8,0},{25,9},{17,25},{1,17},{9,1},{26,10},{1... | collective-permute-start | bytes 3538952 | tf_op jit(solution)/shard_map/ppermute | solution.py:425
  373.4 76.6 %collective-permute-start.39 = (bf16[144,32,128]{2,1,0:T(8,128)(2,1)S(1)}, bf16[144,32,128]{2,1,0:T(8,128)(2,1)}, u32[]{:S(2)}, u32[]{:S(2)}) collective-permute-start(bf16[144,32,128]{2,1,0:T(8,128)(2,1)S(1)} %get-tuple-element.1218), channel_id=1, source_target_pairs={{8,24},{24,16},{16,0},{0,8},{9,25},{25,17},{17,1},{1,9},{10,26},{2... | collective-permute-start | bytes 3538952 | tf_op jit(solution)/shard_map/ppermute | solution.py:425
  435.6 245.2 %reduce-scatter.9.cloned.1.call-start = ((), (), s32[]{:S(2)}) async-start(), calls=%async_computation.6 | async-start | bytes 1179648 | tf_op jit(solution)/shard_map/reduce_scatter | solution.py:728
  449.3 27.8 %collective-permute-start.45 = (bf16[144,32,128]{2,1,0:T(8,128)(2,1)}, bf16[144,32,128]{2,1,0:T(8,128)(2,1)S(1)}, u32[]{:S(2)}, u32[]{:S(2)}) collective-permute-start(bf16[144,32,128]{2,1,0:T(8,128)(2,1)} %dynamic_slice.540), channel_id=1, source_target_pairs={{24,8},{16,24},{0,16},{8,0},{25,9},{17,25},{1,17},{9,1},{26,10},{1... | collective-permute-start | bytes 3538952 | tf_op jit(solution)/shard_map/ppermute | solution.py:425
  458.3 27.6 %collective-permute-start.40 = (bf16[144,32,128]{2,1,0:T(8,128)(2,1)}, bf16[144,32,128]{2,1,0:T(8,128)(2,1)S(1)}, u32[]{:S(2)}, u32[]{:S(2)}) collective-permute-start(bf16[144,32,128]{2,1,0:T(8,128)(2,1)} %dynamic_slice.536), channel_id=1, source_target_pairs={{8,24},{24,16},{16,0},{0,8},{9,25},{25,17},{17,1},{1,9},{10,26},{2... | collective-permute-start | bytes 3538952 | tf_op jit(solution)/shard_map/ppermute | solution.py:425
  480.8 27.0 %collective-permute-start.46 = (bf16[144,32,128]{2,1,0:T(8,128)(2,1)}, bf16[144,32,128]{2,1,0:T(8,128)(2,1)S(1)}, u32[]{:S(2)}, u32[]{:S(2)}) collective-permute-start(bf16[144,32,128]{2,1,0:T(8,128)(2,1)} %dynamic_slice.541), channel_id=1, source_target_pairs={{24,8},{16,24},{0,16},{8,0},{25,9},{17,25},{1,17},{9,1},{26,10},{1... | collective-permute-start | bytes 3538952 | tf_op jit(solution)/shard_map/ppermute | solution.py:425
  489.6 26.9 %collective-permute-start.41 = (bf16[144,32,128]{2,1,0:T(8,128)(2,1)}, bf16[144,32,128]{2,1,0:T(8,128)(2,1)}, u32[]{:S(2)}, u32[]{:S(2)}) collective-permute-start(bf16[144,32,128]{2,1,0:T(8,128)(2,1)} %dynamic_slice.537), channel_id=1, source_target_pairs={{8,24},{24,16},{16,0},{0,8},{9,25},{25,17},{17,1},{1,9},{10,26},{2... | collective-permute-start | bytes 3538952 | tf_op jit(solution)/shard_map/ppermute | solution.py:425
  511.6 26.3 %collective-permute-start.47 = (bf16[144,32,128]{2,1,0:T(8,128)(2,1)}, bf16[144,32,128]{2,1,0:T(8,128)(2,1)S(1)}, u32[]{:S(2)}, u32[]{:S(2)}) collective-permute-start(bf16[144,32,128]{2,1,0:T(8,128)(2,1)} %dynamic_slice.542), channel_id=1, source_target_pairs={{24,8},{16,24},{0,16},{8,0},{25,9},{17,25},{1,17},{9,1},{26,10},{1... | collective-permute-start | bytes 3538952 | tf_op jit(solution)/shard_map/ppermute | solution.py:425
  521.5 26.0 %collective-permute-start.42 = (bf16[144,32,128]{2,1,0:T(8,128)(2,1)}, bf16[144,32,128]{2,1,0:T(8,128)(2,1)S(1)}, u32[]{:S(2)}, u32[]{:S(2)}) collective-permute-start(bf16[144,32,128]{2,1,0:T(8,128)(2,1)} %dynamic_slice.538), channel_id=1, source_target_pairs={{8,24},{24,16},{16,0},{0,8},{9,25},{25,17},{17,1},{1,9},{10,26},{2... | collective-permute-start | bytes 3538952 | tf_op jit(solution)/shard_map/ppermute | solution.py:425
  647.7 81.4 %all-gather.26.cloned.1.call-start = ((), (), s32[]{:S(2)}) async-start(), calls=%async_computation.9 | async-start | bytes 4718592 | tf_op jit(solution)/shard_map/all_gather | solution.py:735
  683.8 132.2 %reduce-scatter.11.cloned.1.call-start = ((), (), s32[]{:S(2)}) async-start(), calls=%async_computation.7 | async-start | bytes 4718592 | tf_op jit(solution)/shard_map/reduce_scatter | solution.py:654
  767.1 459.5 %all-gather.28.cloned.1.call-start = ((), (), s32[]{:S(2)}) async-start(), calls=%async_computation.10 | async-start | bytes 19021824 | tf_op jit(solution)/shard_map/all_gather | solution.py:800
  849.2 378.4 %all-gather.30.cloned.1.call-start = ((), (), s32[]{:S(2)}) async-start(), calls=%async_computation.11 | async-start | bytes 14155776 | tf_op jit(solution)/shard_map/all_gather | solution.py:799
  893.6 26.6 %collective-permute-start.54 = (bf16[144,32,128]{2,1,0:T(8,128)(2,1)}, bf16[144,32,128]{2,1,0:T(8,128)(2,1)}, u32[]{:S(2)}, u32[]{:S(2)}) collective-permute-start(bf16[144,32,128]{2,1,0:T(8,128)(2,1)} %dynamic_slice.463), channel_id=1, source_target_pairs={{24,8},{16,24},{0,16},{8,0},{25,9},{17,25},{1,17},{9,1},{26,10},{1... | collective-permute-start | bytes 3538952 | tf_op jit(solution)/shard_map/ppermute | solution.py:437
  896.7 29.8 %collective-permute-start.49 = (bf16[144,32,128]{2,1,0:T(8,128)(2,1)S(1)}, bf16[144,32,128]{2,1,0:T(8,128)(2,1)}, u32[]{:S(2)}, u32[]{:S(2)}) collective-permute-start(bf16[144,32,128]{2,1,0:T(8,128)(2,1)S(1)} %dynamic_slice.453), channel_id=1, source_target_pairs={{8,24},{24,16},{16,0},{0,8},{9,25},{25,17},{17,1},{1,9},{10,26},{2... | collective-permute-start | bytes 3538952 | tf_op jit(solution)/shard_map/ppermute | solution.py:437
  924.7 25.7 %collective-permute-start.55 = (bf16[144,32,128]{2,1,0:T(8,128)(2,1)S(1)}, bf16[144,32,128]{2,1,0:T(8,128)(2,1)}, u32[]{:S(2)}, u32[]{:S(2)}) collective-permute-start(bf16[144,32,128]{2,1,0:T(8,128)(2,1)S(1)} %dynamic_slice.548), channel_id=1, source_target_pairs={{24,8},{16,24},{0,16},{8,0},{25,9},{17,25},{1,17},{9,1},{26,10},{1... | collective-permute-start | bytes 3538952 | tf_op jit(solution)/shard_map/ppermute | solution.py:437
  1341.8 119.1 %collective-permute-start.70 = (bf16[256,8,128]{2,1,0:T(8,128)(2,1)S(1)}, bf16[256,8,128]{2,1,0:T(8,128)(2,1)}, u32[]{:S(2)}, u32[]{:S(2)}) collective-permute-start(bf16[256,8,128]{2,1,0:T(8,128)(2,1)S(1)} %bitcast.490), channel_id=1, source_target_pairs={{0,16},{8,24},{16,0},{24,8},{1,17},{9,25},{17,1},{25,9},{2,18},{10... | collective-permute-start | bytes 1572872 | tf_op jit(solution)/shard_map/ppermute | solution.py:842
  1342.9 90.3 %collective-permute-start.69 = (bf16[256,8,128]{2,1,0:T(8,128)(2,1)S(1)}, bf16[256,8,128]{2,1,0:T(8,128)(2,1)}, u32[]{:S(2)}, u32[]{:S(2)}) collective-permute-start(bf16[256,8,128]{2,1,0:T(8,128)(2,1)S(1)} %bitcast.491), channel_id=1, source_target_pairs={{0,8},{8,16},{16,24},{24,0},{1,9},{9,17},{17,25},{25,1},{2,10},{10... | collective-permute-start | bytes 1572872 | tf_op jit(solution)/shard_map/ppermute | solution.py:842
  1343.0 145.8 %collective-permute-start.71 = (bf16[256,8,128]{2,1,0:T(8,128)(2,1)S(1)}, bf16[256,8,128]{2,1,0:T(8,128)(2,1)}, u32[]{:S(2)}, u32[]{:S(2)}) collective-permute-start(bf16[256,8,128]{2,1,0:T(8,128)(2,1)S(1)} %bitcast.492), channel_id=1, source_target_pairs={{0,24},{8,0},{16,8},{24,16},{1,25},{9,1},{17,9},{25,17},{2,26},{10... | collective-permute-start | bytes 1572872 | tf_op jit(solution)/shard_map/ppermute | solution.py:842
  1351.0 165.5 %collective-permute-start.79 = (bf16[104,32,128]{2,1,0:T(8,128)(2,1)S(1)}, bf16[104,32,128]{2,1,0:T(8,128)(2,1)S(1)}, u32[]{:S(2)}, u32[]{:S(2)}) collective-permute-start(bf16[104,32,128]{2,1,0:T(8,128)(2,1)S(1)} %dynamic_slice.565), channel_id=1, source_target_pairs={{24,8},{16,24},{0,16},{8,0},{25,9},{17,25},{1,17},{9,1},{26,10},{1... | collective-permute-start | bytes 2555912 | tf_op jit(solution)/shard_map/ppermute | solution.py:437
  1358.1 160.6 %collective-permute-start.75 = (bf16[104,32,128]{2,1,0:T(8,128)(2,1)}, bf16[104,32,128]{2,1,0:T(8,128)(2,1)}, u32[]{:S(2)}, u32[]{:S(2)}) collective-permute-start(bf16[104,32,128]{2,1,0:T(8,128)(2,1)} %dynamic_slice.562), channel_id=1, source_target_pairs={{8,24},{24,16},{16,0},{0,8},{9,25},{25,17},{17,1},{1,9},{10,26},{2... | collective-permute-start | bytes 2555912 | tf_op jit(solution)/shard_map/ppermute | solution.py:437
  1579.4 26.5 %collective-permute-start.81 = (f32[8,128]{1,0:T(8,128)S(1)}, f32[8,128]{1,0:T(8,128)S(1)}, u32[]{:S(2)}, u32[]{:S(2)}) collective-permute-start(f32[8,128]{1,0:T(8,128)S(1)} %add.1779), channel_id=1, source_target_pairs={{0,2},{1,3},{2,0},{3,1},{4,6},{5,7},{6,4},{7,5},{8,10},{9,11},{10,... | collective-permute-start | bytes 12296 | tf_op jit(solution)/shard_map/ppermute | solution.py:462
  1610.4 27.2 %collective-permute-start.83 = (f32[8,128]{1,0:T(8,128)S(1)}, f32[8,128]{1,0:T(8,128)S(1)}, u32[]{:S(2)}, u32[]{:S(2)}) collective-permute-start(f32[8,128]{1,0:T(8,128)S(1)} %add.1781), channel_id=1, source_target_pairs={{0,8},{8,0},{16,24},{24,16},{1,9},{9,1},{17,25},{25,17},{2,10},{10... | collective-permute-start | bytes 12296 | tf_op jit(solution)/shard_map/ppermute | solution.py:462
  (159 other events, 2884.9 us)
Sparse Core Ops, SparseCore 0:
  138.8 51.0 reduce-scatter.4
  286.3 47.1 all-gather.23
  435.7 49.8 reduce-scatter.6
  647.8 32.9 reduce-scatter.8
  684.0 45.0 all-gather.25
  767.3 48.7 reduce-scatter.10
  849.4 150.6 all-gather.27
  1001.7 114.8 all-gather.29
